TPU v7x, 32 devices: a whole 2x2x4 slice. The times are simulated.
32 devices in a mesh: dp: 8 (over z, y), tp: 4 (over x, core).
Axes of the slice: x: 2, y: 2, z: 4, core: 2. Of those that a mesh axis runs over, the one named last changes fastest.
Arguments:
- tokens: bfloat16 [128, 256, 512], P('dp'), may hold values from -6 to 6
- frame_counts: int32 [128], P('dp'), may hold values from 128 to 256, as said below
- rate_groups: int32 [128], P('dp'), may hold values from 0 to 1
- conv_weight: bfloat16 [7, 512], replicated, may hold values from -2 to 2
- conv_bias: bfloat16 [512], replicated, may hold values from -3 to 3
- norm_scale: bfloat16 [2, 512], replicated, may hold values from 0.5 to 1.5
- norm_shift: bfloat16 [2, 512], replicated, may hold values from -2 to 2
- weight_in: bfloat16 [512, 1536], P(None, 'tp'), may hold values from -0.25 to 0.25
- bias_in: bfloat16 [1536], P('tp'), may hold values from -2 to 2
- weight_out: bfloat16 [1536, 512], P('tp'), may hold values from -0.21875 to 0.21875
- bias_out: bfloat16 [512], replicated, may hold values from -2 to 2
- layer_scale: bfloat16 [512], replicated, may hold values from 0.5 to 1.5
- cotangent: bfloat16 [128, 256, 512], P('dp'), may hold values from -6 to 6
Outputs:
- block_out: bfloat16 [128, 256, 512], P('dp')
- grad_tokens: float32 [128, 256, 512], P('dp')
- grad_conv_weight: float32 [7, 512], replicated
- grad_conv_bias: float32 [512], replicated
- grad_norm_scale: float32 [2, 512], replicated
- grad_norm_shift: float32 [2, 512], replicated
- grad_weight_in: float32 [512, 1536], P(None, 'tp')
- grad_bias_in: float32 [1536], P('tp')
- grad_weight_out: float32 [1536, 512], P('tp')
- grad_bias_out: float32 [512], replicated
- grad_layer_scale: float32 [512], replicated
Inputs may be any that keep to these rules, and one draw needn't show every extreme that they name: `frame_counts`: an item of group 0 has at most 256 live frames, one of group 1 at most 240; both bounds are reached, and so is the least.
All inputs are finite; a program needn't handle non-finite values.
Results may differ from a plain program's by a relative error of at most 0.0061.
Values may be sent and summed in bfloat16 or wider, within the bound.
No kernel may reach another device: no remote copies, remote signals or barrier semaphores. Data moves between devices by JAX's collectives and lax.ppermute only.
A program may use at most 192 MiB of HBM per device.

v0:
```python
import jax
import jax.numpy as jnp
from jax import lax
from jax.sharding import PartitionSpec as P

EPS = 1e-06
HIGH = lax.Precision.HIGHEST


def gelu_parts(pre_act):
    normal_cdf = 0.5 * (1.0 + lax.erf(pre_act * 0.7071067811865476))
    density = jnp.exp(-0.5 * pre_act * pre_act) * 0.3989422804014327
    return (pre_act * normal_cdf, normal_cdf + pre_act * density)


def contract_rows(left, right, precision=None):
    return lax.dot_general(
        left,
        right,
        (((0,), (0,)), ((), ())),
        precision=precision,
        preferred_element_type=jnp.float32,
    )


def contract_last(left, right):
    return lax.dot_general(
        left, right, (((1,), (1,)), ((), ())), preferred_element_type=jnp.float32
    )


def per_device(
    tokens,
    frame_counts,
    rate_groups,
    conv_weight,
    conv_bias,
    norm_scale,
    norm_shift,
    weight_in,
    bias_in,
    weight_out,
    bias_out,
    layer_scale,
    cotangent,
):
    item_count, frames, model_width = tokens.shape
    row_count = item_count * frames
    tap_count = conv_weight.shape[0]
    half_width = tap_count // 2
    rate_count = norm_scale.shape[0]
    frame_mask = (jnp.arange(frames)[None, :] < frame_counts[:, None]).astype(jnp.float32)
    masked = tokens.astype(jnp.float32) * frame_mask[..., None]
    padded = jnp.pad(masked, ((0, 0), (half_width, half_width), (0, 0)))
    conv_taps = conv_weight.astype(jnp.float32)
    conv = conv_bias.astype(jnp.float32) + conv_taps[0] * padded[:, 0:frames]
    for tap_index in range(1, tap_count):
        conv = conv + conv_taps[tap_index] * padded[:, tap_index : tap_index + frames]
    row_mean = jnp.mean(conv, axis=-1, keepdims=True)
    centered = conv - row_mean
    variance = jnp.mean(centered * centered, axis=-1, keepdims=True)
    inv_std = lax.rsqrt(variance + EPS).reshape(row_count, 1)
    normed = centered.reshape(row_count, model_width) * inv_std
    hot_items = (rate_groups[:, None] == jnp.arange(rate_count)[None, :]).astype(jnp.float32)
    hot_rows = jnp.broadcast_to(hot_items[:, None, :], (item_count, frames, rate_count)).reshape(
        row_count, rate_count
    )
    scale_table = norm_scale.astype(jnp.float32)
    shift_table = norm_shift.astype(jnp.float32)
    scale_items = jnp.dot(hot_items, scale_table, precision=HIGH)
    shift_items = jnp.dot(hot_items, shift_table, precision=HIGH)
    adapted = (
        (
            normed.reshape(item_count, frames, model_width) * scale_items[:, None, :]
            + shift_items[:, None, :]
        )
        .astype(jnp.bfloat16)
        .reshape(row_count, model_width)
    )
    pre_act = jnp.dot(adapted, weight_in, preferred_element_type=jnp.float32) + bias_in.astype(
        jnp.float32
    )
    activation, gelu_slope = gelu_parts(pre_act)
    act_low = activation.astype(jnp.bfloat16)
    masked_rows = masked.reshape(row_count, model_width)
    mask_rows = frame_mask.reshape(row_count, 1)
    grad_rows = cotangent.astype(jnp.float32).reshape(row_count, model_width) * mask_rows
    gamma = layer_scale.astype(jnp.float32)
    bias_last = bias_out.astype(jnp.float32)
    summed = lax.psum(jnp.dot(act_low, weight_out, preferred_element_type=jnp.float32), "tp")
    branch = summed + bias_last
    out_rows = ((masked_rows + gamma * branch) * mask_rows).astype(jnp.bfloat16)
    grad_gamma = jnp.sum(grad_rows * branch, axis=0)
    grad_bias_last = jnp.sum(grad_rows * gamma, axis=0)
    branch_low = (grad_rows * gamma).astype(jnp.bfloat16)
    grad_weight_out = contract_rows(act_low, branch_low)
    act_grad = contract_last(branch_low, weight_out)
    pre_grad = act_grad * gelu_slope
    grad_bias_in = jnp.sum(pre_grad, axis=0)
    pre_low = pre_grad.astype(jnp.bfloat16)
    grad_weight_in = contract_rows(adapted, pre_low)
    adapted_grad = lax.psum(contract_last(pre_low, weight_in), "tp")
    grad_scale = contract_rows(hot_rows, adapted_grad * normed, HIGH)
    grad_shift = contract_rows(hot_rows, adapted_grad, HIGH)
    normed_grad = adapted_grad * jnp.dot(hot_rows, scale_table, precision=HIGH)
    mean_grad = jnp.mean(normed_grad, axis=-1, keepdims=True)
    mean_cross = jnp.mean(normed_grad * normed, axis=-1, keepdims=True)
    conv_grad = inv_std * (normed_grad - mean_grad - normed * mean_cross)
    grad_conv_bias = jnp.sum(conv_grad, axis=0)
    tap_grads = []
    for tap_index in range(tap_count):
        shifted = padded[:, tap_index : tap_index + frames].reshape(row_count, model_width)
        tap_grads.append(jnp.sum(conv_grad * shifted, axis=0))
    grad_conv_weight = jnp.stack(tap_grads, axis=0)
    grad_padded = jnp.pad(
        conv_grad.reshape(item_count, frames, model_width),
        ((0, 0), (half_width, half_width), (0, 0)),
    )
    masked_grad = conv_taps[0] * grad_padded[:, 2 * half_width : 2 * half_width + frames]
    for tap_index in range(1, tap_count):
        offset = 2 * half_width - tap_index
        masked_grad = masked_grad + conv_taps[tap_index] * grad_padded[:, offset : offset + frames]
    grad_tokens = frame_mask[..., None] * (
        grad_rows.reshape(item_count, frames, model_width) + masked_grad
    )
    (
        grad_weight_in,
        grad_bias_in,
        grad_weight_out,
        grad_conv_weight,
        grad_conv_bias,
        grad_scale,
        grad_shift,
        grad_bias_last,
        grad_gamma,
    ) = lax.psum(
        (
            grad_weight_in,
            grad_bias_in,
            grad_weight_out,
            grad_conv_weight,
            grad_conv_bias,
            grad_scale,
            grad_shift,
            grad_bias_last,
            grad_gamma,
        ),
        "dp",
    )
    block_out = out_rows.reshape(item_count, frames, model_width)
    return (
        block_out,
        grad_tokens,
        grad_conv_weight,
        grad_conv_bias,
        grad_scale,
        grad_shift,
        grad_weight_in,
        grad_bias_in,
        grad_weight_out,
        grad_bias_last,
        grad_gamma,
    )


def solution(mesh):
    in_specs = (
        P("dp", None, None),
        P("dp"),
        P("dp"),
        P(),
        P(),
        P(),
        P(),
        P(None, "tp"),
        P("tp"),
        P("tp", None),
        P(),
        P(),
        P("dp", None, None),
    )
    out_specs = (
        P("dp", None, None),
        P("dp", None, None),
        P(),
        P(),
        P(),
        P(),
        P(None, "tp"),
        P("tp"),
        P("tp", None),
        P(),
        P(),
    )
    return jax.shard_map(
        per_device, mesh=mesh, in_specs=in_specs, out_specs=out_specs, check_vma=False
    )
```

profile of v0, /device:TPU:0, one launch (start us, length us, event | category | flops | bytes accessed | tf_op | source)
XLA Modules:
  0.0 496.8 jit_solution(17823976869492066244)
XLA Ops:
  7.2 0.0 copy-start
  7.2 0.0 all-reduce.10.cloned.1.call-start
  7.2 0.0 copy-start.6
  7.3 1.0 fusion.34
  8.3 0.0 copy-start.23
  8.3 0.0 copy-start.25
  8.3 0.0 copy-start.27
  8.3 0.0 copy-start.29
  8.3 1.0 fusion.24
  9.3 0.7 convert_element_type.68
  10.0 2.6 convert_multiply_fusion
  12.6 21.1 %fusion.33 = (f32[16,256]{1,0:T(8,128)S(1)}, f32[16,256,512]{2,1,0:T(8,128)}, f32[16,256,512]{2,1,0:T(8,128)}, f32[16,256,512]{2,1,0:T(8,128)}, f32[16,256,512]{...) fusion(f32[512]{0:T(512)S(1)} %bitcast.116, f32[512]{0:T(512)S(1)} %bitcast.114, ...), kind=kLoop, calls=%fused_computation.75 | loop fusion | flops 35647488 | bytes 71352320 | tf_op jit(solution)/shard_map/reduce_sum | solution.py:59
  33.7 0.0 copy-done.19
  33.8 0.0 copy-start.33
  33.8 0.0 copy-start.35
  33.8 0.0 copy-start.31
  33.8 0.0 copy-start.37
  33.8 0.0 copy-start.38
  33.9 4.2 multiply_reduce_fusion.3
  38.1 0.7 fusion.30
  38.7 0.0 copy-done.33
  38.7 0.2 fusion.26
  38.9 0.2 fusion.27
  39.2 0.0 copy-start.15
  39.2 1.3 add_convert_fusion
  40.5 0.0 copy-start.8
  40.5 0.0 copy-start.5
  40.5 2.9 multiply_convert_fusion.1
  43.5 0.0 copy-start.11
  43.5 1.0 copy-done.5
  44.5 1.1 multiply_convert_fusion
  45.6 5.0 %fusion.35 = (f32[384]{0:T(512)}, bf16[4096,384]{1,0:T(8,128)(2,1)S(1)}) fusion(f32[4096,384]{1,0:T(8,128)S(1)} %get-tuple-element.70, bf16[4096,512]{1,0:T(8,128)(2,1)S(1)} %multiply_convert_fusion, bf16[384,512]{1,0:T(8,128)(2,1)S(1)} %copy-done.11), kind=kOutput, calls=%fused_computation.77 | convolution fusion | flops 1627913856 | bytes 14026240 | tf_op jit(solution)/shard_map/dot_general | solution.py:27
  50.7 5.6 %fusion.21 = f32[4096,512]{1,0:T(8,128)} fusion(bf16[512,384]{1,0:T(8,128)(2,1)S(1)} %copy-done, bf16[4096,384]{1,0:T(8,128)(2,1)S(1)} %get-tuple-element.73), kind=kOutput, calls=%fused_computation.56 | convolution fusion | flops 1610612736 | bytes 11927552 | tf_op jit(solution)/shard_map/dot_general | solution.py:27
  56.3 5.7 %fusion.36 = f32[4096,512]{1,0:T(8,128)} fusion(bf16[4096,384]{1,0:T(8,128)(2,1)S(1)} %get-tuple-element.69, bf16[384,512]{1,0:T(8,128)(2,1)S(1)} %copy-done.11), kind=kOutput, calls=%fused_computation.78 | convolution fusion | flops 1610612736 | bytes 11927552 | tf_op jit(solution)/shard_map/dot_general | solution.py:90
  62.0 0.0 all-reduce.10.cloned.1.call-update
  62.1 0.2 all-reduce.8.cloned.1.call-start
  62.3 0.0 copy-start.9
  62.3 6.0 %fusion.38 = f32[384,512]{1,0:T(8,128)} fusion(bf16[4096,384]{1,0:T(8,128)(2,1)} %copy-done.10, bf16[4096,512]{1,0:T(8,128)(2,1)} %copy-done.7), kind=kOutput, calls=%fused_computation.80 | convolution fusion | flops 1610612736 | bytes 8126464 | tf_op jit(solution)/shard_map/dot_general | solution.py:17
  68.3 0.0 copy-start.32
  68.3 3.2 fusion.19
  71.5 0.0 all-reduce.8.cloned.1.call-update
  71.6 0.0 copy-done.14
  71.6 0.1 broadcast_bitcast_fusion
  71.7 282.0 %all-reduce.10.cloned.1.call-done = (f32[4096,512]{1,0:T(8,128)}, f32[4096,512]{1,0:T(8,128)}) async-done(((f32[4096,512]{1,0:T(8,128)}, f32[4096,512]{1,0:T(8,128)}), (f32[4096,512]{1,0:T(8,128)}, f32[4096,512]{1,0:T(8,128)})) %all-reduce.10.cloned.1.call-update) | async-done | bytes 16777232 | tf_op jit(solution)/shard_map/psum | solution.py:90
  353.8 7.1 %fusion.37 = f32[2,512]{1,0:T(2,128)S(1)} fusion(f32[4096,2]{0,1:T(2,128)S(1)} %bitcast.97, f32[4096,512]{1,0:T(8,128)} %get-tuple-element.31), kind=kOutput, calls=%fused_computation.79 | convolution fusion | flops 50331648 | bytes 8425472 | tf_op jit(solution)/shard_map/dot_general | solution.py:17
  360.9 0.0 copy-done.32
  360.9 0.0 copy-start.16
  360.9 11.0 %fusion.32 = (f32[4096]{0:T(1024)S(1)}, f32[4096]{0:T(1024)S(1)}, f32[4096,512]{1,0:T(8,128)}) fusion(f32[4096]{0:T(1024)S(1)} %bitcast.102, f32[16,256,512]{2,1,0:T(8,128)} %copy-done.2, f32[4096,512]{1,0:T(8,128)S(1)} %copy-done.4, f32[4096,2]{0,1:T(2,128)S(1)} %bitcast.98, bf16[2,512]{1,0:T(2,128)(2,1)S(1)} %copy-done.32), kind=kOutput, calls=%fused_computation.74 | convolution fusion | flops 60809216 | bytes 25249792 | tf_op jit(solution)/shard_map/dot_general | solution.py:105
  372.0 37.2 %multiply_reduce_fusion = (f32[512]{0:T(512)S(1)}, bf16[4096,512]{1,0:T(8,128)(2,1)}, f32[4096,512]{1,0:T(8,128)}, f32[512]{0:T(512)S(1)}, f32[512]{0:T(512)S(1)...) fusion(bf16[16,256,512]{2,1,0:T(8,128)(2,1)} %param.25, ...), kind=kLoop, calls=%fused_computation.20 | loop fusion | flops 60812800 | bytes 109139968 | tf_op jit(solution)/shard_map/reduce_sum | solution.py:93
  409.2 0.0 copy-start.24
  409.2 0.0 copy-start.26
  409.2 0.0 copy-start.28
  409.2 0.0 copy-start.30
  409.2 8.1 %fusion.9 = f32[2,512]{1,0:T(2,128)S(1)} fusion(f32[4096,2]{0,1:T(2,128)S(1)} %bitcast.99, f32[4096,512]{1,0:T(8,128)} %get-tuple-element.31, f32[4096,512]{1,0:T(8,128)} %get-tuple-element.40), kind=kOutput, calls=%fused_computation.22 | convolution fusion | flops 52428800 | bytes 16814080 | tf_op jit(solution)/shard_map/dot_general | solution.py:17
  417.4 0.0 copy-start.1
  417.4 0.0 copy-done.18
  417.4 0.0 copy-done.20
  417.4 0.0 copy-done.22
  417.5 0.0 copy-done.24
  417.5 0.0 copy-start.36
  417.5 30.6 %multiply_reduce_fusion.1 = (f32[512]{0:T(512)S(1)}, f32[16,256,512]{2,1,0:T(8,128)}) fusion(bf16[16,256,512]{2,1,0:T(8,128)(2,1)} %param.25, f32[512]{0:T(512)S(1)} %copy-done.16, f32[16,256]{1,0:T(8,128)S(1)} %get-tuple-element.68, f32[512]{0:T(512)S(1)} %bitcast.117, f32[512]{0:T(512)S(1)} %bitcast.115, f32[512]{0:T(512)S(1)} %bitcast.113, ...), kind=kLoop, calls=%fused_computation.21 | loop fusion | flops 39845376 | bytes 21006336 | tf_op jit(solution)/shard_map/reduce_sum | solution.py:94
  448.1 37.7 %all-reduce.2 = (f32[7,512]{1,0:T(8,128)}, f32[512]{0:T(512)}, f32[2,512]{1,0:T(2,128)}, f32[2,512]{1,0:T(2,128)}, f32[384]{0:T(512)}, /*index=5*/f32[512]{0:T(512)}, f32[512]{0:T(512)}) all-reduce(f32[7,512]{1,0:T(8,128)S(1)} %stack.31, f32[512]{0:T(512)S(1)} %get-tuple-element.48, ...), channel_id=1, replica_groups=mesh['dp'=8,'tp'=4] {'dp'}, use_global_device_ids=true, to_apply=%region_13.14 | all-reduce | flops 7552 | bytes 60416 | tf_op jit(solution)/shard_map/psum | solution.py:136
  485.8 2.1 copy.31
  487.9 2.1 copy.32
  (58 shorter events, 0.2 us)
Async XLA Ops:
  7.2 33.4 %copy-start = (bf16[512,384]{1,0:T(8,128)(2,1)S(1)}, bf16[512,384]{1,0:T(8,128)(2,1)}, u32[]{:S(2)}) copy-start(bf16[512,384]{1,0:T(8,128)(2,1)} %param.20) | copy-start | bytes 1179652
  7.2 346.6 %all-reduce.10.cloned.1.call-start = ((), (), s32[]{:S(2)}) async-start(), calls=%async_computation.1 | async-start | bytes 33554432 | tf_op jit(solution)/shard_map/psum | solution.py:90
  7.2 5.4 %copy-start.6 = (bf16[16,256,512]{2,1,0:T(8,128)(2,1)S(1)}, bf16[16,256,512]{2,1,0:T(8,128)(2,1)}, u32[]{:S(2)}) copy-start(bf16[16,256,512]{2,1,0:T(8,128)(2,1)} %param.13) | copy-start | bytes 12582916
  8.2 25.5 %copy-start.17 = (f32[1,512]{1,0:T(1,128)}, f32[1,512]{1,0:T(1,128)S(1)}, u32[]{:S(2)}) copy-start(f32[1,512]{1,0:T(1,128)S(1)} %get-tuple-element.60) | copy-start | bytes 6148
  8.2 25.5 %copy-start.19 = (f32[1,512]{1,0:T(1,128)}, f32[1,512]{1,0:T(1,128)S(1)}, u32[]{:S(2)}) copy-start(f32[1,512]{1,0:T(1,128)S(1)} %get-tuple-element.61) | copy-start | bytes 6148
  8.2 25.5 %copy-start.21 = (f32[1,512]{1,0:T(1,128)}, f32[1,512]{1,0:T(1,128)S(1)}, u32[]{:S(2)}) copy-start(f32[1,512]{1,0:T(1,128)S(1)} %get-tuple-element.62) | copy-start | bytes 6148
  8.3 25.5 %copy-start.23 = (f32[1,512]{1,0:T(1,128)}, f32[1,512]{1,0:T(1,128)S(1)}, u32[]{:S(2)}) copy-start(f32[1,512]{1,0:T(1,128)S(1)} %get-tuple-element.63) | copy-start | bytes 6148
  8.3 25.5 %copy-start.25 = (f32[1,512]{1,0:T(1,128)}, f32[1,512]{1,0:T(1,128)S(1)}, u32[]{:S(2)}) copy-start(f32[1,512]{1,0:T(1,128)S(1)} %get-tuple-element.64) | copy-start | bytes 6148
  8.3 25.5 %copy-start.27 = (f32[1,512]{1,0:T(1,128)}, f32[1,512]{1,0:T(1,128)S(1)}, u32[]{:S(2)}) copy-start(f32[1,512]{1,0:T(1,128)S(1)} %get-tuple-element.65) | copy-start | bytes 6148
  8.3 25.5 %copy-start.29 = (f32[1,512]{1,0:T(1,128)}, f32[1,512]{1,0:T(1,128)S(1)}, u32[]{:S(2)}) copy-start(f32[1,512]{1,0:T(1,128)S(1)} %get-tuple-element.66) | copy-start | bytes 6148
  12.6 21.2 %copy-start.3 = (f32[16,256,512]{2,1,0:T(8,128)}, f32[16,256,512]{2,1,0:T(8,128)S(1)}, u32[]{:S(2)}) copy-start(f32[16,256,512]{2,1,0:T(8,128)S(1)} %convert_multiply_fusion) | copy-start | bytes 25165828
  33.8 4.9 copy-start.33
  33.8 4.9 copy-start.35
  33.8 5.1 %copy-start.31 = (bf16[2,512]{1,0:T(2,128)(2,1)S(1)}, bf16[2,512]{1,0:T(2,128)(2,1)}, u32[]{:S(2)}) copy-start(bf16[2,512]{1,0:T(2,128)(2,1)} %param.18) | copy-start | bytes 6148
  33.8 5.3 %copy-start.37 = (bf16[384]{0:T(512)(128)(2,1)S(1)}, bf16[384]{0:T(512)(128)(2,1)}, u32[]{:S(2)}) copy-start(bf16[384]{0:T(512)(128)(2,1)} %param.21) | copy-start | bytes 2308
  33.8 5.3 %copy-start.38 = (bf16[512]{0:T(512)(128)(2,1)S(1)}, bf16[512]{0:T(512)(128)(2,1)}, u32[]{:S(2)}) copy-start(bf16[512]{0:T(512)(128)(2,1)} %param.24) | copy-start | bytes 3076
  38.1 5.4 %copy-start.2 = (f32[16,256,512]{2,1,0:T(8,128)}, f32[16,256,512]{2,1,0:T(8,128)S(1)}, u32[]{:S(2)}) copy-start(f32[16,256,512]{2,1,0:T(8,128)S(1)} %get-tuple-element.34) | copy-start | bytes 25165828
  39.2 4.4 copy-start.12
  39.2 4.3 copy-start.15
  40.5 3.0 copy-start.8
  40.5 4.0 copy-start.5
  43.5 12.8 %copy-start.10 = (bf16[4096,384]{1,0:T(8,128)(2,1)}, bf16[4096,384]{1,0:T(8,128)(2,1)S(1)}, u32[]{:S(2)}) copy-start(bf16[4096,384]{1,0:T(8,128)(2,1)S(1)} %get-tuple-element.69) | copy-start | bytes 9437188
  43.5 2.1 copy-start.11
  45.6 5.1 %copy-start.7 = (bf16[4096,512]{1,0:T(8,128)(2,1)}, bf16[4096,512]{1,0:T(8,128)(2,1)S(1)}, u32[]{:S(2)}) copy-start(bf16[4096,512]{1,0:T(8,128)(2,1)S(1)} %multiply_convert_fusion) | copy-start | bytes 12582916
  62.1 423.8 %all-reduce.8.cloned.1.call-start = ((), (), s32[]{:S(2)}) async-start(), calls=%async_computation | async-start | bytes 3145728 | tf_op jit(solution)/shard_map/psum | solution.py:136
  62.3 6.0 %copy-start.9 = (bf16[16,256,512]{2,1,0:T(8,128)(2,1)S(1)}, bf16[16,256,512]{2,1,0:T(8,128)(2,1)}, u32[]{:S(2)}) copy-start(bf16[16,256,512]{2,1,0:T(8,128)(2,1)} %copy-done.8) | copy-start | bytes 12582916
  68.3 3.3 copy-start.34
  68.3 3.3 copy-start.14
  68.3 3.4 copy-start.39
  68.3 292.6 %copy-start.32 = (bf16[2,512]{1,0:T(2,128)(2,1)S(1)}, bf16[2,512]{1,0:T(2,128)(2,1)}, u32[]{:S(2)}) copy-start(bf16[2,512]{1,0:T(2,128)(2,1)} %param.18) | copy-start | bytes 6148
  353.7 7.1 %copy-start.4 = (f32[4096,512]{1,0:T(8,128)S(1)}, f32[4096,512]{1,0:T(8,128)}, u32[]{:S(2)}) copy-start(f32[4096,512]{1,0:T(8,128)} %get-tuple-element.31) | copy-start | bytes 25165828
  360.9 11.1 %copy-start.13 = (f32[2,2,8,128]{3,1,2,0:T(2,128)S(1)}, f32[2,2,8,128]{3,1,2,0:T(2,128)}, u32[]{:S(2)}) copy-start(f32[2,2,8,128]{3,1,2,0:T(2,128)} %copy-done.12) | copy-start | bytes 49156
  360.9 11.0 %copy-start.16 = (f32[512]{0:T(512)S(1)}, f32[512]{0:T(512)}, u32[]{:S(2)}) copy-start(f32[512]{0:T(512)} %copy-done.15) | copy-start | bytes 6148
  409.2 8.3 %copy-start.18 = (f32[1,512]{1,0:T(1,128)S(1)}, f32[1,512]{1,0:T(1,128)}, u32[]{:S(2)}) copy-start(f32[1,512]{1,0:T(1,128)} %copy-done.17) | copy-start | bytes 6148
  409.2 8.3 %copy-start.20 = (f32[1,512]{1,0:T(1,128)S(1)}, f32[1,512]{1,0:T(1,128)}, u32[]{:S(2)}) copy-start(f32[1,512]{1,0:T(1,128)} %copy-done.19) | copy-start | bytes 6148
  409.2 8.3 %copy-start.22 = (f32[1,512]{1,0:T(1,128)S(1)}, f32[1,512]{1,0:T(1,128)}, u32[]{:S(2)}) copy-start(f32[1,512]{1,0:T(1,128)} %copy-done.21) | copy-start | bytes 6148
  409.2 8.3 %copy-start.24 = (f32[1,512]{1,0:T(1,128)S(1)}, f32[1,512]{1,0:T(1,128)}, u32[]{:S(2)}) copy-start(f32[1,512]{1,0:T(1,128)} %copy-done.23) | copy-start | bytes 6148
  409.2 8.3 %copy-start.26 = (f32[1,512]{1,0:T(1,128)S(1)}, f32[1,512]{1,0:T(1,128)}, u32[]{:S(2)}) copy-start(f32[1,512]{1,0:T(1,128)} %copy-done.25) | copy-start | bytes 6148
  409.2 8.3 %copy-start.28 = (f32[1,512]{1,0:T(1,128)S(1)}, f32[1,512]{1,0:T(1,128)}, u32[]{:S(2)}) copy-start(f32[1,512]{1,0:T(1,128)} %copy-done.27) | copy-start | bytes 6148
  409.2 8.3 %copy-start.30 = (f32[1,512]{1,0:T(1,128)S(1)}, f32[1,512]{1,0:T(1,128)}, u32[]{:S(2)}) copy-start(f32[1,512]{1,0:T(1,128)} %copy-done.29) | copy-start | bytes 6148
  417.4 72.5 %copy-start.1 = (bf16[512,384]{1,0:T(8,128)(2,1)S(1)}, bf16[512,384]{1,0:T(8,128)(2,1)}, u32[]{:S(2)}) copy-start(bf16[512,384]{1,0:T(8,128)(2,1)} %param.20) | copy-start | bytes 1179652
  417.5 30.6 %copy-start.36 = (f32[384]{0:T(512)S(1)}, f32[384]{0:T(512)}, u32[]{:S(2)}) copy-start(f32[384]{0:T(512)} %get-tuple-element.72) | copy-start | bytes 4612
Sparse Core Ops, SparseCore 0:
  62.2 291.5 all-reduce.9
  358.5 89.2 all-reduce.7
where the time goes:
time: 497 us
  waiting for transfers between devices  282 us (57%)
  other arithmetic  100 us (20%)
  matrix products  55.2 us (11%)
  blocking collectives  37.7 us (8%)
  between operations  14.7 us (3%)
  local copies, waits for them, and re-layouts  6.43 us (1%)
    psum x1, waiting for transfers between devices, per_device(): lax.psum(jnp.dot(act_low, weight_out, preferred_element_type=jnp.float32)...  282 us
    psum x1, blocking collectives, per_device(): lax.psum((grad_weight_in, grad_bias_in, grad_weight_out, grad_conv_weight...  37.7 us
    reduce_sum x1, other arithmetic, per_device(): grad_gamma = jnp.sum(grad_rows * branch, axis=0)  37.2 us
    reduce_sum x1, other arithmetic, per_device(): grad_bias_last = jnp.sum(grad_rows * gamma, axis=0)  30.6 us
    dot_general x4, matrix products, contract_rows(): lax.dot_general(left, right, (((0,), (0,)), ((), ())), precision=precisio...  24.5 us
    reduce_sum x1, other arithmetic, per_device(): row_mean = jnp.mean(conv, axis=-1, keepdims=True)  21.1 us
    dot_general x1, matrix products, per_device(): normed_grad = adapted_grad * jnp.dot(hot_rows, scale_table, precision=HIGH)  11 us
    dot_general x2, matrix products, contract_last(): lax.dot_general(left, right, (((1,), (1,)), ((), ())), preferred_element_...  10.6 us
  transfers between devices with their start and end apart: 2, of which 1 were waited for; matrix products, arithmetic and copies ran while one was open for 21% of the time, Pallas kernels for 0%

commit v1 on v0

v1 whole, which is shorter than its diff:
```python
import functools
import jax
import jax.numpy as jnp
from jax import lax
from jax.experimental import pallas as pl
from jax.experimental.pallas import tpu as pltpu
from jax.sharding import PartitionSpec as P

EPS = 1e-06
BF, F32 = jnp.bfloat16, jnp.float32
TILE = 256
VMEM_LIMIT = 60 * 1024 * 1024
PAD = 8


def fold(x):
    return jnp.sum(x.reshape(x.shape[0] // 8, 8, x.shape[1]), axis=0)


def gelu_parts(pre):
    cdf = 0.5 + 0.5 * lax.erf(pre * 0.7071067811865476)
    density = jnp.exp(-0.5 * pre * pre) * 0.3989422804014327
    return pre * cdf, cdf + pre * density


def pick(table, group):
    rows = table[...].astype(F32)
    value = rows[0:1]
    for r in range(1, rows.shape[0]):
        value = jnp.where(group == r, rows[r:r + 1], value)
    return value


def dot(a, b):
    return jnp.dot(a, b, preferred_element_type=F32)


def dot_t(a, b):
    return lax.dot_general(a, b, (((1,), (1,)), ((), ())), preferred_element_type=F32)


def dot_rows(a, b):
    return lax.dot_general(a, b, (((0,), (0,)), ((), ())), preferred_element_type=F32)


def conv_norm_kernel(n, taps, chunk, meta, tok, cot, cw, cb, ns, nsh, gamma,
                     adapted, normed, inv, low, gbo, pad):
    j = pl.program_id(0)
    frames = tok.shape[1]
    width = tok.shape[2]
    half = taps // 2
    count = meta[n + j]
    group = meta[2 * n + j]
    off = meta[3 * n + j]

    @pl.when(j == 0)
    def _():
        gbo[...] = jnp.zeros_like(gbo)
        pad[0:PAD, :] = jnp.zeros((PAD, width), F32)
        pad[PAD + frames:, :] = jnp.zeros((pad.shape[0] - PAD - frames, width), F32)

    rows = lax.broadcasted_iota(jnp.int32, (frames, 1), 0)
    pad[PAD:PAD + frames, :] = jnp.where(rows < count, tok[0].astype(F32), 0.0)
    scale = pick(ns, group)
    shift = pick(nsh, group)
    gam = gamma[...].astype(F32)
    bias = cb[...].astype(F32)
    w = cw[...].astype(F32)

    def step(i, acc):
        r0 = pl.multiple_of(i * chunk, chunk)
        live = (lax.broadcasted_iota(jnp.int32, (chunk, 1), 0) + r0) < count
        slab = pad[pl.ds(r0, chunk + 2 * PAD), :]
        conv = bias + w[0:1] * slab[PAD - half:PAD - half + chunk]
        for k in range(1, taps):
            s = PAD - half + k
            conv = conv + w[k:k + 1] * slab[s:s + chunk]
        mean = jnp.mean(conv, axis=-1, keepdims=True)
        cent = conv - mean
        var = jnp.mean(cent * cent, axis=-1, keepdims=True)
        istd = lax.rsqrt(var + EPS)
        nrm = cent * istd
        dst = pl.ds(pl.multiple_of(off + r0, 16), chunk)
        adapted[dst, :] = (nrm * scale + shift).astype(BF)
        normed[dst, :] = nrm.astype(BF)
        inv[dst, :] = jnp.broadcast_to(istd, (chunk, 128))
        bg = jnp.where(live, cot[0, pl.ds(r0, chunk), :].astype(F32), 0.0) * gam
        low[dst, :] = bg.astype(BF)
        return acc + fold(bg)

    gbo[...] += lax.fori_loop(0, pl.cdiv(count, chunk), step, jnp.zeros((8, width), F32))

    @pl.when(j == n - 1)
    def _():
        end = pl.ds(pl.multiple_of(meta[4 * n], 16), TILE)
        adapted[end, :] = jnp.zeros((TILE, width), BF)
        low[end, :] = jnp.zeros((TILE, width), BF)


def conv_norm(meta, tok, cot, cw, cb, ns, nsh, gamma, n, chunk=32):
    items, frames, width = tok.shape
    taps = cw.shape[0]
    rows = n * frames + TILE
    def whole(shape):
        return pl.BlockSpec(shape, lambda j, m: (0,) * len(shape))
    item = pl.BlockSpec((1, frames, width), lambda j, m: (m[j], 0, 0))
    return pl.pallas_call(
        functools.partial(conv_norm_kernel, n, taps, chunk),
        grid_spec=pltpu.PrefetchScalarGridSpec(
            num_scalar_prefetch=1, grid=(n,),
            in_specs=[item, item, whole(cw.shape), whole(cb.shape), whole(ns.shape), whole(nsh.shape), whole(gamma.shape)],
            out_specs=[whole((rows, width)), whole((rows, width)), whole((rows, 128)), whole((rows, width)), whole((8, width))],
            scratch_shapes=[pltpu.VMEM((frames + 2 * PAD, width), F32)]),
        out_shape=[jax.ShapeDtypeStruct((rows, width), BF), jax.ShapeDtypeStruct((rows, width), BF),
                   jax.ShapeDtypeStruct((rows, 128), F32), jax.ShapeDtypeStruct((rows, width), BF),
                   jax.ShapeDtypeStruct((8, width), F32)],
        compiler_params=pltpu.CompilerParams(dimension_semantics=("arbitrary",), vmem_limit_bytes=VMEM_LIMIT),
    )(meta, tok, cot, cw, cb, ns, nsh, gamma)


def hidden_kernel(n, meta, ad, low, wib_a, wib_b, wo_a, wo_b, act, pre_low, keep, send, gbi, win, wout, dwo, dwi):
    t = pl.program_id(0)
    width, h = wib_a.shape[0] - 16, wib_a.shape[1]

    @pl.when(t == 0)
    def _():
        win[:, :h] = wib_a[...]
        win[:, h:] = wib_b[...]
        wout[:h, :] = wo_a[...]
        wout[h:, :] = wo_b[...]
        dwo[...] = jnp.zeros_like(dwo)
        dwi[...] = jnp.zeros_like(dwi)
        gbi[...] = jnp.zeros_like(gbi)

    @pl.when(t < meta[4 * n + 1])
    def _():
        a, b = ad[...], low[...]
        activation, slope = gelu_parts(dot(a, win[:width, :]) + win[width:width + 1, :].astype(F32))
        grad = dot_t(b, wout[...]) * slope
        lo = activation.astype(BF)
        act[...] = lo
        dwo[...] += dot_rows(lo, b)
        gbi[...] += fold(grad)
        g = grad.astype(BF)
        pre_low[...] = g
        dwi[...] += dot_rows(a, g)

    @pl.when(t == pl.num_programs(0) - 1)
    def _():
        for side, dst in ((0, keep), (1, send)):
            for q in range(width // 128):
                dst[q * h:(q + 1) * h, :] = dwo[side * h:(side + 1) * h, q * 128:(q + 1) * 128]
            base = width // 128 * h
            for q in range(h // 128):
                lane = side * h + q * 128
                dst[base + q * width:base + (q + 1) * width, :] = dwi[:, lane:lane + 128]


def hidden(meta, ad, low, wib_a, wib_b, wo_a, wo_b, n, tile=TILE):
    rows, width = ad.shape
    h = wib_a.shape[1]
    tiles = (rows - TILE) // tile
    packed = 2 * width * h // 128
    def whole(shape):
        return pl.BlockSpec(shape, lambda t, m: (0,) * len(shape))
    def tiled(cols):
        return pl.BlockSpec((tile, cols), lambda t, m: (jnp.minimum(t, m[4 * n + 1] - 1), 0))
    return pl.pallas_call(
        functools.partial(hidden_kernel, n),
        grid_spec=pltpu.PrefetchScalarGridSpec(
            num_scalar_prefetch=1, grid=(tiles,),
            in_specs=[tiled(width), tiled(width), whole(wib_a.shape), whole(wib_a.shape), whole(wo_a.shape), whole(wo_a.shape)],
            out_specs=[tiled(2 * h), tiled(2 * h), whole((packed, 128)), whole((packed, 128)), whole((8, 2 * h))],
            scratch_shapes=[pltpu.VMEM((width + 16, 2 * h), BF), pltpu.VMEM((2 * h, width), BF),
                            pltpu.VMEM((2 * h, width), F32), pltpu.VMEM((width, 2 * h), F32)]),
        out_shape=[jax.ShapeDtypeStruct((rows, 2 * h), BF), jax.ShapeDtypeStruct((rows, 2 * h), BF),
                   jax.ShapeDtypeStruct((packed, 128), F32), jax.ShapeDtypeStruct((packed, 128), F32),
                   jax.ShapeDtypeStruct((8, 2 * h), F32)],
        compiler_params=pltpu.CompilerParams(dimension_semantics=("arbitrary",), vmem_limit_bytes=VMEM_LIMIT),
    )(meta, ad, low, wib_a, wib_b, wo_a, wo_b)


def mix_kernel(n, meta, ad, low, act_own, pre_own, wia, wib, woa, wob, wic, wid, woc, wod, bout, branch, ag,
               wi1, wo1, wi2, wo2):
    t = pl.program_id(0)
    width, h = wia.shape[0] - 16, wia.shape[1]

    @pl.when(t == 0)
    def _():
        for dst, a, b in ((wi1, wia, wib), (wi2, wic, wid)):
            dst[:, :h] = a[...]
            dst[:, h:] = b[...]
        for dst, a, b in ((wo1, woa, wob), (wo2, woc, wod)):
            dst[:h, :] = a[...]
            dst[h:, :] = b[...]

    @pl.when(t < meta[4 * n + 1])
    def _():
        a, b = ad[...], low[...]
        activation, slope = gelu_parts(dot(a, wi2[:width, :]) + wi2[width:width + 1, :].astype(F32))
        grad = dot_t(b, wo2[...]) * slope
        branch[...] = (dot(act_own[...], wo1[...]) + dot(activation.astype(BF), wo2[...])) + bout[...].astype(F32)
        ag[...] = dot_t(pre_own[...], wi1[:width, :]) + dot_t(grad.astype(BF), wi2[:width, :])


def mix(meta, ad, low, act_own, pre_own, w8, bout, n, tile=TILE):
    rows, width = ad.shape
    h2 = act_own.shape[1]
    tiles = (rows - TILE) // tile
    def whole(shape):
        return pl.BlockSpec(shape, lambda t, m: (0,) * len(shape))
    def tiled(cols):
        return pl.BlockSpec((tile, cols), lambda t, m: (jnp.minimum(t, m[4 * n + 1] - 1), 0))
    return pl.pallas_call(
        functools.partial(mix_kernel, n),
        grid_spec=pltpu.PrefetchScalarGridSpec(
            num_scalar_prefetch=1, grid=(tiles,),
            in_specs=[tiled(width), tiled(width), tiled(h2), tiled(h2)] + [whole(w.shape) for w in w8] + [whole((1, width))],
            out_specs=[tiled(width), tiled(width)],
            scratch_shapes=[pltpu.VMEM((width + 16, h2), BF), pltpu.VMEM((h2, width), BF)] * 2),
        out_shape=[jax.ShapeDtypeStruct((rows, width), F32), jax.ShapeDtypeStruct((rows, width), F32)],
        compiler_params=pltpu.CompilerParams(dimension_semantics=("arbitrary",), vmem_limit_bytes=VMEM_LIMIT),
    )(meta, ad, low, act_own, pre_own, *w8, bout)


def finish_kernel(n, taps, chunk, meta, tok, cot, branch, ag, normed, inv, cw, ns, gamma,
                  out, gtok, sums, cgp):
    j = pl.program_id(0)
    frames, width = tok.shape[1], tok.shape[2]
    half = taps // 2
    count = meta[n + j]
    group = meta[2 * n + j]
    off = meta[3 * n + j]
    rates = ns.shape[0]

    @pl.when(j == 0)
    def _():
        sums[...] = jnp.zeros_like(sums)
        cgp[...] = jnp.zeros_like(cgp)

    scale = pick(ns, group)
    gam = gamma[...].astype(F32)
    w = cw[...].astype(F32)
    zero = jnp.zeros((8, width), F32)
    steps = pl.cdiv(count, chunk)

    def step(i, accs):
        a_cb, a_ls, a_sc, a_sh = accs
        r0 = pl.multiple_of(i * chunk, chunk)
        live = (lax.broadcasted_iota(jnp.int32, (chunk, 1), 0) + r0) < count
        src = pl.ds(pl.multiple_of(off + r0, 16), chunk)
        br = jnp.where(live, branch[src, :], 0.0)
        tk = tok[0, pl.ds(r0, chunk), :].astype(F32)
        back = jnp.where(live, cot[0, pl.ds(r0, chunk), :].astype(F32), 0.0)
        out[0, pl.ds(r0, chunk), :] = jnp.where(live, tk + gam * br, 0.0).astype(BF)
        g = jnp.where(live, ag[src, :], 0.0)
        nr = normed[src, :].astype(F32)
        gn = g * nr
        ng = g * scale
        m1 = jnp.mean(ng, axis=-1, keepdims=True)
        m2 = jnp.mean(ng * nr, axis=-1, keepdims=True)
        cg = inv[src, 0:1] * (ng - m1 - nr * m2)
        cgp[pl.ds(pl.multiple_of(PAD + r0, 8), chunk), :] = cg
        return a_cb + fold(cg), a_ls + fold(back * br), a_sc + fold(gn), a_sh + fold(g)

    a_cb, a_ls, a_sc, a_sh = lax.fori_loop(0, steps, step, (zero,) * 4)
    sums[taps] += a_cb
    sums[taps + 1] += a_ls
    sums[taps + 2 + group] += a_sc
    sums[taps + 2 + rates + group] += a_sh
    def clear(i, _):
        r0 = pl.multiple_of(i * chunk, chunk)
        out[0, pl.ds(r0, chunk), :] = jnp.zeros((chunk, width), BF)
        gtok[0, pl.ds(r0, chunk), :] = jnp.zeros((chunk, width), gtok.dtype)
        cgp[pl.ds(pl.multiple_of(PAD + r0, 8), chunk), :] = jnp.zeros((chunk, width), F32)
        return 0
    lax.fori_loop(steps, frames // chunk, clear, 0)

    for q in range(width // 128):
        lanes = slice(q * 128, q * 128 + 128)
        wq = w[:, lanes]

        def conv_step(i, accs):
            r0 = pl.multiple_of(i * chunk, chunk)
            live = (lax.broadcasted_iota(jnp.int32, (chunk, 1), 0) + r0) < count
            slab = cgp[pl.ds(r0, chunk + 2 * PAD), lanes]
            tk = jnp.where(live, tok[0, pl.ds(r0, chunk), lanes].astype(F32), 0.0)
            total = cot[0, pl.ds(r0, chunk), lanes].astype(F32)
            new = []
            for k in range(taps):
                s = PAD + half - k
                sh = slab[s:s + chunk]
                total = total + wq[k:k + 1] * sh
                new.append(accs[k] + fold(tk * sh))
            gtok[0, pl.ds(r0, chunk), lanes] = jnp.where(live, total, 0.0).astype(gtok.dtype)
            return tuple(new)

        accs = lax.fori_loop(0, steps, conv_step, (jnp.zeros((8, 128), F32),) * taps)
        for k in range(taps):
            sums[k, :, lanes] += accs[k]


def finish(meta, tok, cot, branch, ag, normed, inv, cw, ns, gamma, n, chunk=32, gt_dtype=BF):
    items, frames, width = tok.shape
    taps = cw.shape[0]
    rates = ns.shape[0]
    n_sums = taps + 2 + 2 * rates
    rows = branch.shape[0]
    def whole(shape):
        return pl.BlockSpec(shape, lambda j, m: (0,) * len(shape))
    item = pl.BlockSpec((1, frames, width), lambda j, m: (m[j], 0, 0))
    own = pl.BlockSpec((1, frames, width), lambda j, m: (j, 0, 0))
    return pl.pallas_call(
        functools.partial(finish_kernel, n, taps, chunk),
        grid_spec=pltpu.PrefetchScalarGridSpec(
            num_scalar_prefetch=1, grid=(n,),
            in_specs=[item, item, whole((rows, width)), whole((rows, width)), whole((rows, width)), whole((rows, 128)),
                      whole(cw.shape), whole(ns.shape), whole(gamma.shape)],
            out_specs=[own, own, whole((n_sums, 8, width))],
            scratch_shapes=[pltpu.VMEM((frames + 2 * PAD, width), F32)]),
        out_shape=[jax.ShapeDtypeStruct((n, frames, width), BF), jax.ShapeDtypeStruct((n, frames, width), gt_dtype),
                   jax.ShapeDtypeStruct((n_sums, 8, width), F32)],
        compiler_params=pltpu.CompilerParams(dimension_semantics=("arbitrary",), vmem_limit_bytes=VMEM_LIMIT),
    )(meta, tok, cot, branch, ag, normed, inv, cw, ns, gamma)


def swap(x, step):
    size = lax.axis_size("tp")
    return lax.ppermute(x, "tp", [(i, i ^ step) for i in range(size)])


def exchange(x):
    return lax.all_to_all(x, "dp", 0, 0)


def per_device(tokens, frame_counts, rate_groups, conv_weight, conv_bias, norm_scale, norm_shift,
               weight_in, bias_in, weight_out, bias_out, layer_scale, cotangent):
    items, frames, width = tokens.shape
    taps, rates = conv_weight.shape[0], norm_scale.shape[0]
    quarter = weight_in.shape[1]
    n = items // 2
    dp = lax.axis_size("dp")
    core = lax.axis_index("tp") % 2

    wib = jnp.concatenate([weight_in, jnp.broadcast_to(bias_in[None], (16, quarter))], axis=0)
    wib_b, wo_b = swap(wib, 1), swap(weight_out, 1)
    wib_c, wo_c = swap(wib, 2), swap(weight_out, 2)
    wib_d, wo_d = swap(wib_c, 1), swap(wo_c, 1)

    own = core * n + jnp.arange(n, dtype=jnp.int32)
    counts = lax.dynamic_slice(frame_counts, (core * n,), (n,))
    groups = lax.dynamic_slice(rate_groups, (core * n,), (n,))
    sizes = (counts + 15) // 16 * 16
    ends = jnp.cumsum(sizes)
    total = ends[n - 1:]
    meta = jnp.concatenate([own, counts, groups, ends - sizes, total, (total + TILE - 1) // TILE]).astype(jnp.int32)

    row = lambda v: v[None, :]
    adapted, normed, inv, low, gbo = conv_norm(
        meta, tokens, cotangent, conv_weight, row(conv_bias), norm_scale, norm_shift, row(layer_scale), n)
    act, pre_low, keep, send, gbi = hidden(meta, adapted, low, wib, wib_b, weight_out, wo_b, n)
    grads = (keep + swap(send, 1)).astype(BF)
    shard = exchange(grads.reshape(dp, grads.shape[0] // dp, 128))

    branch, ag = mix(meta, adapted, low, act, pre_low,
                     (wib, wib_b, weight_out, wo_b, wib_c, wib_d, wo_c, wo_d), row(bias_out), n)
    out, gtok, sums = finish(meta, tokens, cotangent, branch, ag, normed, inv, conv_weight, norm_scale,
                             row(layer_scale), n)

    out_b, gtok_b = swap(out, 1), swap(gtok, 1)
    first = core == 0

    def join(a, b):
        return jnp.where(first, jnp.concatenate([a, b]), jnp.concatenate([b, a]))

    block_out = join(out, out_b)
    grad_tokens = join(gtok, gtok_b).astype(F32)

    small = jnp.concatenate([jnp.sum(sums, axis=1), jnp.sum(gbo, axis=0, keepdims=True)], axis=0)
    gb = jnp.sum(gbi, axis=0)
    gb_keep, gb_send = gb[:quarter], gb[quarter:]
    fill = jnp.zeros((width - quarter,), F32)
    small_send = jnp.concatenate([small, row(jnp.concatenate([gb_send, fill]))], axis=0)
    small_keep = jnp.concatenate([small, row(jnp.concatenate([gb_keep, fill]))], axis=0)
    small = small_keep + swap(small_send, 1)
    count = small.shape[0]
    small = jnp.pad(small, ((0, -count % 4), (0, 0))).reshape(-1, 128)
    high = lax.reduce_precision(small, 8, 7)
    part = jnp.concatenate([high.astype(BF), (small - high).astype(BF)], axis=0)

    mine = jnp.sum(shard.astype(F32), axis=0).astype(BF)
    message = jnp.concatenate([mine, part], axis=0)
    message = exchange(jnp.broadcast_to(message[None], (dp,) + message.shape))
    m = mine.shape[0]
    full = message[:, :m].reshape(dp * m, 128).astype(F32)
    both = jnp.sum(message[:, m:].astype(F32), axis=0)
    k = both.shape[0] // 2
    small = (both[:k] + both[k:]).reshape(-1, width)
    wq, hq = width // 128, quarter // 128
    cut = wq * quarter
    grad_weight_out = full[:cut].reshape(wq, quarter, 128).transpose(1, 0, 2).reshape(quarter, width)
    grad_weight_in = full[cut:].reshape(hq, width, 128).transpose(1, 0, 2).reshape(width, quarter)
    return (
        block_out,
        grad_tokens,
        small[:taps],
        small[taps],
        small[taps + 2:taps + 2 + rates],
        small[taps + 2 + rates:taps + 2 + 2 * rates],
        grad_weight_in,
        small[taps + 3 + 2 * rates, :quarter],
        grad_weight_out,
        small[taps + 2 + 2 * rates],
        small[taps + 1],
    )


def solution(mesh):
    items, copied = P("dp", None, None), P()
    in_specs = (items, P("dp"), P("dp"), copied, copied, copied, copied, P(None, "tp"), P("tp"), P("tp", None), copied, copied, items)
    out_specs = (items, items, copied, copied, copied, copied, P(None, "tp"), P("tp"), P("tp", None), copied, copied)
    return jax.shard_map(per_device, mesh=mesh, in_specs=in_specs, out_specs=out_specs, check_vma=False)
```

time: 497 us -> 155 us (0.31)
  waiting for transfers between devices: 282 us -> 30.3 us
  other arithmetic: 100 us -> 15.5 us
  Pallas kernels: 0 us -> 73.3 us
  matrix products: 55.2 us -> 0 us
  blocking collectives: 37.7 us -> 0 us
  starting transfers between devices: 0.26 us -> 20.2 us
  between operations: 14.7 us -> 1.59 us
  local copies, waits for them, and re-layouts: 6.43 us -> 15.2 us
    psum x2 -> x0, waiting for transfers between devices: 282 us -> none  [the longest x1 282 us: per_device(): lax.psum(jnp.dot(act_low, weight_out, preferred_element_type=jnp.float32)...]
    reduce_sum x4 -> x5, other arithmetic: 93.1 us -> 1.31 us  [the longest x1 1.13 us: per_device(): jnp.sum(sums, axis=1)]
    pallas_call x0 -> x4, Pallas kernels: none -> 73.3 us  [the longest x1 24.9 us: finish(): pl.pallas_call(functools.partial(finish_kernel, n, taps, chunk), grid_spe...]
    dot_general x11 -> x0, matrix products: 55.2 us -> none  [the longest x4 24.5 us: contract_rows(): lax.dot_general(left, right, (((0,), (0,)), ((), ())), precision=precisio...]
    psum x1 -> x0, blocking collectives: 37.7 us -> none  [per_device(): lax.psum((grad_weight_in, grad_bias_in, grad_weight_out, grad_conv_weight...]
    all_to_all x0 -> x2, waiting for transfers between devices: none -> 16.6 us  [exchange(): return lax.all_to_all(x, 'dp', 0, 0)]
    all_to_all x0 -> x2, starting transfers between devices: none -> 15.6 us  [exchange(): return lax.all_to_all(x, 'dp', 0, 0)]
    ppermute x0 -> x10, waiting for transfers between devices: none -> 13.7 us  [swap(): return lax.ppermute(x, 'tp', [(i, i ^ step) for i in range(size)])]
  transfers between devices with their start and end apart: 2 -> 12, of which waited for: 1 -> 4; matrix products, arithmetic and copies ran while one was open for 21% -> 14% of each run, Pallas kernels for 0% -> 39%
where the time goes in v1:
time: 155 us; the launch traced here: 156 us
  Pallas kernels  73.3 us (47%)
  waiting for transfers between devices  30.3 us (20%)
  starting transfers between devices  20.2 us (13%)
  other arithmetic  15.5 us (10%)
  local copies, waits for them, and re-layouts  15.2 us (10%)
  between operations  1.59 us (1%)
    pallas_call x1, Pallas kernels, finish(): pl.pallas_call(functools.partial(finish_kernel, n, taps, chunk), grid_spe...  24.9 us
    pallas_call x1, Pallas kernels, conv_norm(): pl.pallas_call(functools.partial(conv_norm_kernel, n, taps, chunk), grid_...  20.2 us
    all_to_all x2, waiting for transfers between devices, exchange(): return lax.all_to_all(x, 'dp', 0, 0)  16.6 us
    all_to_all x2, starting transfers between devices, exchange(): return lax.all_to_all(x, 'dp', 0, 0)  15.6 us
    pallas_call x1, Pallas kernels, mix(): pl.pallas_call(functools.partial(mix_kernel, n), grid_spec=pltpu.Prefetch...  15.3 us
    ppermute x10, waiting for transfers between devices, swap(): return lax.ppermute(x, 'tp', [(i, i ^ step) for i in range(size)])  13.7 us
    pallas_call x1, Pallas kernels, hidden(): pl.pallas_call(functools.partial(hidden_kernel, n), grid_spec=pltpu.Prefe...  12.9 us
    convert_element_type x1, other arithmetic, per_device(): grad_tokens = join(gtok, gtok_b).astype(F32)  5.47 us
  transfers between devices with their start and end apart: 12, of which 4 were waited for; matrix products, arithmetic and copies ran while one was open for 14% of the time, Pallas kernels for 39%

profile of v1, /device:TPU:0, one launch (start us, length us, event | category | flops | bytes accessed | tf_op | source)
XLA Modules:
  0.0 156.0 jit_solution(8910824965753225319)
XLA Ops:
  0.6 0.7 broadcast_in_dim.34
  1.3 1.0 pad_maximum_fusion.wib_a.wia
  2.4 0.0 copy-start
  2.4 0.5 collective-permute-start
  2.9 0.1 collective-permute-start.1
  3.0 0.7 fusion.2
  3.7 0.2 reduce-window.4
  3.9 0.6 slice.66
  5.1 0.7 dynamic_slice.7
  5.9 1.3 broadcast_in_dim.33.gamma
  7.1 1.3 broadcast_in_dim.32.cb
  8.4 1.2 concatenate.36.meta
  9.6 20.2 %shard_map.212 = (bf16[2304,512]{1,0:T(8,128)(2,1)}, bf16[2304,512]{1,0:T(8,128)(2,1)}, f32[2304,128]{1,0:T(8,128)}, bf16[2304,512]{1,0:T(8,128)(2,1)}, f32[8,512]{1,0:T(8,128)}) custom-call(s32[34]{0:T(128)} %concatenate.36.meta, bf16[16,256,512]{2,1,0:T(8,128)(2,1)} %tok.3, bf16[16,256,512]{2,1,0:T(8,128)(2,1)} %cot.3, bf16[7,512]{1,0:T(8,128)(2,1)} %cw.3, ...), custom_call_target="tpu_custom_call" | custom-call | tf_op jit(solution)/shard_map/pallas_call | solution.py:107
  29.8 0.0 collective-permute-done.1.wo_b.wob
  29.8 0.0 collective-permute-done.wib_b.wib
  29.9 0.7 copy-done.5
  30.6 0.1 copy-done.3
  30.7 12.9 %shard_map.213 = (bf16[2304,768]{1,0:T(8,128)(2,1)}, bf16[2304,768]{1,0:T(8,128)(2,1)}, f32[3072,128]{1,0:T(8,128)}, f32[3072,128]{1,0:T(8,128)}, f32[8,768]{1,0:T(8,128)}) custom-call(s32[34]{0:T(128)} %concatenate.36.meta, bf16[2304,512]{1,0:T(8,128)(2,1)} %get-tuple-element.26.ad, bf16[2304,512]{1,0:T(8,128)(2,1)} %get-tuple-element.27.low, ...), custom_call_target="tpu_custom_call" | custom-call | tf_op jit(solution)/shard_map/pallas_call | solution.py:168
  43.6 0.0 copy-start.12
  43.6 0.5 collective-permute-start.8
  44.1 2.6 %collective-permute-start.2 = (bf16[528,384]{1,0:T(8,128)(2,1)}, bf16[528,384]{1,0:T(8,128)(2,1)S(1)}, u32[]{:S(2)}, u32[]{:S(2)}) collective-permute-start(bf16[528,384]{1,0:T(8,128)(2,1)} %copy-done), channel_id=1, source_target_pairs={{0,2},{1,3},{2,0},{3,1},{4,6},{5,7},{6,4},{7,5},{8,10},{9,11},{10,... | collective-permute-start | bytes 1216520 | tf_op jit(solution)/shard_map/ppermute | solution.py:329
  46.7 0.1 collective-permute-start.4
  46.8 10.3 %collective-permute-done.2.wic = bf16[528,384]{1,0:T(8,128)(2,1)S(1)} collective-permute-done((bf16[528,384]{1,0:T(8,128)(2,1)}, bf16[528,384]{1,0:T(8,128)(2,1)S(1)}, u32[]{:S(2)}, u32[]{:S(2)}) %collective-permute-start.2) | collective-permute-done | bytes 405536 | tf_op jit(solution)/shard_map/ppermute | solution.py:329
  57.1 0.0 collective-permute-start.3
  57.1 0.0 collective-permute-done.8
  57.1 2.6 %add_convert_fusion = bf16[3072,128]{1,0:T(8,128)(2,1)} fusion(f32[3072,128]{1,0:T(8,128)} %get-tuple-element.36, f32[3072,128]{1,0:T(8,128)S(1)} %collective-permute-done.8), kind=kLoop, calls=%fused_computation.3 | loop fusion | flops 786432 | bytes 3932160 | tf_op jit(solution)/shard_map/convert_element_type | solution.py:362
  59.7 6.9 %all-to-all-start = ((bf16[8,384,128]{2,1,0:T(8,128)(2,1)}), bf16[8,384,128]{2,1,0:T(8,128)(2,1)S(1)}, u32[]{:S(2)}, u32[]{:S(2)}) async-start(bf16[8,384,128]{2,1,0:T(8,128)(2,1)} %bitcast.3), calls=%async_computation | async-start | bytes 1572864 | tf_op jit(solution)/shard_map/all_to_all | solution.py:333
  66.7 0.0 collective-permute-done.4.woc
  66.7 0.1 collective-permute-start.5
  66.8 0.0 copy-done.12
  66.8 0.6 broadcast_in_dim.35.bout
  67.4 1.1 collective-permute-done.5.wod
  68.5 0.0 collective-permute-done.3.wid
  68.5 0.0 copy-done.8
  68.5 0.8 copy-done.9
  69.3 0.1 copy-done.7
  69.4 15.3 %shard_map.214 = (f32[2304,512]{1,0:T(8,128)}, f32[2304,512]{1,0:T(8,128)}) custom-call(s32[34]{0:T(128)} %concatenate.36.meta, bf16[2304,512]{1,0:T(8,128)(2,1)} %get-tuple-element.26.ad, bf16[2304,512]{1,0:T(8,128)(2,1)} %get-tuple-element.27.low, bf16[2304,768]{1,0:T(8,128)(2,1)} %get-tuple-element.28.act_own, ...), custom_call_target="tpu_custom_call" | custom-call | tf_op jit(solution)/shard_map/pallas_call | solution.py:214
  84.7 0.0 copy-start.13
  84.7 24.9 %shard_map.215 = (bf16[8,256,512]{2,1,0:T(8,128)(2,1)}, bf16[8,256,512]{2,1,0:T(8,128)(2,1)}, f32[13,8,512]{2,1,0:T(8,128)}) custom-call(s32[34]{0:T(128)} %concatenate.36.meta, bf16[16,256,512]{2,1,0:T(8,128)(2,1)} %tok.3, bf16[16,256,512]{2,1,0:T(8,128)(2,1)} %cot.3, f32[2304,512]{1,0:T(8,128)} %get-tuple-element.30.branch, ...), custom_call_target="tpu_custom_call" | custom-call | tf_op jit(solution)/shard_map/pallas_call | solution.py:313
  109.6 0.2 collective-permute-start.7
  109.8 1.1 reduce_sum.49
  111.0 0.4 collective-permute-start.9
  111.4 0.2 collective-permute-start.6
  111.6 2.3 %collective-permute-done.9 = f32[15,512]{1,0:T(8,128)S(1)} collective-permute-done((f32[15,512]{1,0:T(8,128)S(1)}, f32[15,512]{1,0:T(8,128)S(1)}, u32[]{:S(2)}, u32[]{:S(2)}) %collective-permute-start.9) | collective-permute-done | bytes 30752 | tf_op jit(solution)/shard_map/ppermute | solution.py:329
  114.0 0.0 all-to-all-done
  114.0 0.1 reduce_sum.48
  114.1 1.1 broadcast_in_dim.39
  115.2 8.6 %all-to-all-start.1 = ((bf16[8,512,128]{2,1,0:T(8,128)(2,1)}), bf16[8,512,128]{2,1,0:T(8,128)(2,1)S(1)}, u32[]{:S(2)}, u32[]{:S(2)}) async-start(bf16[8,512,128]{2,1,0:T(8,128)(2,1)} %broadcast_in_dim.39), calls=%async_computation.1 | async-start | bytes 2097152 | tf_op jit(solution)/shard_map/all_to_all | solution.py:333
  123.9 0.0 collective-permute-done.7
  123.9 5.5 %fusion = f32[16,256,512]{2,1,0:T(8,128)} fusion(bf16[8,256,512]{2,1,0:T(8,128)(2,1)} %collective-permute-done.7, bf16[8,256,512]{2,1,0:T(8,128)(2,1)S(1)} %copy-done.1, pred[]{:T(512)S(6)} %eq.5), kind=kLoop, calls=%fused_computation.2 | loop fusion | flops 8388608 | bytes 12582913 | tf_op jit(solution)/shard_map/convert_element_type | solution.py:377
  129.3 0.0 collective-permute-done.6
  129.4 4.0 %maximum_select_fusion = bf16[16,256,512]{2,1,0:T(8,128)(2,1)} fusion(bf16[8,256,512]{2,1,0:T(8,128)(2,1)} %collective-permute-done.6, bf16[8,256,512]{2,1,0:T(8,128)(2,1)S(1)} %copy-done.2, pred[]{:T(512)S(6)} %eq.5), kind=kLoop, calls=%fused_computation | loop fusion | flops 6291456 | bytes 8388609 | tf_op jit(solution)/shard_map/jit(_where)/select_n | solution.py:374
  133.3 16.6 %all-to-all-done.1 = bf16[8,512,128]{2,1,0:T(8,128)(2,1)S(1)} async-done(((bf16[8,512,128]{2,1,0:T(8,128)(2,1)}), bf16[8,512,128]{2,1,0:T(8,128)(2,1)S(1)}, u32[]{:S(2)}, u32[]{:S(2)}) %all-to-all-start.1) | async-done | bytes 1048608 | tf_op jit(solution)/shard_map/all_to_all | solution.py:333
  150.0 0.6 slice_bitcast_fusion.1
  150.6 0.6 slice.79
  151.2 0.6 slice.77
  151.8 0.6 slice_reduce_fusion
  152.4 0.6 slice.74
  153.0 0.1 slice_convert_fusion
  153.1 0.1 slice_bitcast_fusion
  153.2 0.3 copy.27
  153.5 1.1 copy.29
  154.6 0.3 copy.26
  154.9 1.1 copy.28
  (36 shorter events, 0.2 us)
Async XLA Ops:
  2.4 27.5 %copy-start = (bf16[528,384]{1,0:T(8,128)(2,1)}, bf16[528,384]{1,0:T(8,128)(2,1)S(1)}, u32[]{:S(2)}) copy-start(bf16[528,384]{1,0:T(8,128)(2,1)S(1)} %pad_maximum_fusion.wib_a.wia) | copy-start | bytes 1216516
  2.4 27.5 %collective-permute-start = (bf16[528,384]{1,0:T(8,128)(2,1)S(1)}, bf16[528,384]{1,0:T(8,128)(2,1)S(1)}, u32[]{:S(2)}, u32[]{:S(2)}) collective-permute-start(bf16[528,384]{1,0:T(8,128)(2,1)S(1)} %pad_maximum_fusion.wib_a.wia), channel_id=1, source_target_pairs={{0,1},{1,0},{2,3},{3,2},{4,5},{5,4},{6,7},{7,6},{8,9},{9,8},{10,11... | collective-permute-start | bytes 1216520 | tf_op jit(solution)/shard_map/ppermute | solution.py:329
  2.9 26.9 %collective-permute-start.1 = (bf16[384,512]{1,0:T(8,128)(2,1)}, bf16[384,512]{1,0:T(8,128)(2,1)S(1)}, u32[]{:S(2)}, u32[]{:S(2)}) collective-permute-start(bf16[384,512]{1,0:T(8,128)(2,1)} %woa.1), channel_id=1, source_target_pairs={{0,1},{1,0},{2,3},{3,2},{4,5},{5,4},{6,7},{7,6},{8,9},{9,8},{10,11... | collective-permute-start | bytes 1179656 | tf_op jit(solution)/shard_map/ppermute | solution.py:329
  29.8 16.9 %copy-start.4 = (bf16[384,512]{1,0:T(8,128)(2,1)S(1)}, bf16[384,512]{1,0:T(8,128)(2,1)}, u32[]{:S(2)}) copy-start(bf16[384,512]{1,0:T(8,128)(2,1)} %woa.1) | copy-start | bytes 1179652
  29.8 0.8 copy-start.5
  29.9 0.9 copy-start.3
  43.6 23.2 %copy-start.12 = (bf16[512]{0:T(512)(128)(2,1)S(1)}, bf16[512]{0:T(512)(128)(2,1)}, u32[]{:S(2)}) copy-start(bf16[512]{0:T(512)(128)(2,1)} %param.23) | copy-start | bytes 3076
  43.6 13.5 %collective-permute-start.8 = (f32[3072,128]{1,0:T(8,128)}, f32[3072,128]{1,0:T(8,128)S(1)}, u32[]{:S(2)}, u32[]{:S(2)}) collective-permute-start(f32[3072,128]{1,0:T(8,128)} %get-tuple-element.37), channel_id=1, source_target_pairs={{0,1},{1,0},{2,3},{3,2},{4,5},{5,4},{6,7},{7,6},{8,9},{9,8},{10,11... | collective-permute-start | bytes 4718600 | tf_op jit(solution)/shard_map/ppermute | solution.py:329
  44.1 13.0 %collective-permute-start.2 = (bf16[528,384]{1,0:T(8,128)(2,1)}, bf16[528,384]{1,0:T(8,128)(2,1)S(1)}, u32[]{:S(2)}, u32[]{:S(2)}) collective-permute-start(bf16[528,384]{1,0:T(8,128)(2,1)} %copy-done), channel_id=1, source_target_pairs={{0,2},{1,3},{2,0},{3,1},{4,6},{5,7},{6,4},{7,5},{8,10},{9,11},{10,... | collective-permute-start | bytes 1216520 | tf_op jit(solution)/shard_map/ppermute | solution.py:329
  46.7 20.0 %collective-permute-start.4 = (bf16[384,512]{1,0:T(8,128)(2,1)S(1)}, bf16[384,512]{1,0:T(8,128)(2,1)S(1)}, u32[]{:S(2)}, u32[]{:S(2)}) collective-permute-start(bf16[384,512]{1,0:T(8,128)(2,1)S(1)} %copy-done.4), channel_id=1, source_target_pairs={{0,2},{1,3},{2,0},{3,1},{4,6},{5,7},{6,4},{7,5},{8,10},{9,11},{10,... | collective-permute-start | bytes 1179656 | tf_op jit(solution)/shard_map/ppermute | solution.py:329
  57.1 11.4 %copy-start.6 = (bf16[528,384]{1,0:T(8,128)(2,1)}, bf16[528,384]{1,0:T(8,128)(2,1)S(1)}, u32[]{:S(2)}) copy-start(bf16[528,384]{1,0:T(8,128)(2,1)S(1)} %collective-permute-done.2.wic) | copy-start | bytes 1216516
  57.1 11.3 %collective-permute-start.3 = (bf16[528,384]{1,0:T(8,128)(2,1)S(1)}, bf16[528,384]{1,0:T(8,128)(2,1)S(1)}, u32[]{:S(2)}, u32[]{:S(2)}) collective-permute-start(bf16[528,384]{1,0:T(8,128)(2,1)S(1)} %collective-permute-done.2.wic), channel_id=1, source_target_pairs={{0,1},{1,0},{2,3},{3,2},{4,5},{5,4},{6,7},{7,6},{8,9},{9,8},{10,11... | collective-permute-start | bytes 1216520 | tf_op jit(solution)/shard_map/ppermute | solution.py:329
  59.7 54.2 %all-to-all-start = ((bf16[8,384,128]{2,1,0:T(8,128)(2,1)}), bf16[8,384,128]{2,1,0:T(8,128)(2,1)S(1)}, u32[]{:S(2)}, u32[]{:S(2)}) async-start(bf16[8,384,128]{2,1,0:T(8,128)(2,1)} %bitcast.3), calls=%async_computation | async-start | bytes 1572864 | tf_op jit(solution)/shard_map/all_to_all | solution.py:333
  66.7 1.8 %copy-start.8 = (bf16[384,512]{1,0:T(8,128)(2,1)}, bf16[384,512]{1,0:T(8,128)(2,1)S(1)}, u32[]{:S(2)}) copy-start(bf16[384,512]{1,0:T(8,128)(2,1)S(1)} %collective-permute-done.4.woc) | copy-start | bytes 1179652
  66.7 1.8 %collective-permute-start.5 = (bf16[384,512]{1,0:T(8,128)(2,1)S(1)}, bf16[384,512]{1,0:T(8,128)(2,1)S(1)}, u32[]{:S(2)}, u32[]{:S(2)}) collective-permute-start(bf16[384,512]{1,0:T(8,128)(2,1)S(1)} %collective-permute-done.4.woc), channel_id=1, source_target_pairs={{0,1},{1,0},{2,3},{3,2},{4,5},{5,4},{6,7},{7,6},{8,9},{9,8},{10,11... | collective-permute-start | bytes 1179656 | tf_op jit(solution)/shard_map/ppermute | solution.py:329
  68.5 0.8 copy-start.9
  68.5 0.9 copy-start.7
  84.7 25.1 %copy-start.11 = (f32[8,512]{1,0:T(8,128)S(1)}, f32[8,512]{1,0:T(8,128)}, u32[]{:S(2)}) copy-start(f32[8,512]{1,0:T(8,128)} %get-tuple-element.39) | copy-start | bytes 49156
  84.7 25.1 %copy-start.10 = (f32[8,768]{1,0:T(8,128)S(1)}, f32[8,768]{1,0:T(8,128)}, u32[]{:S(2)}) copy-start(f32[8,768]{1,0:T(8,128)} %get-tuple-element.40) | copy-start | bytes 73732
  84.7 26.9 %copy-start.13 = (pred[512]{0:T(512)(128)(4,1)S(1)}, pred[512]{0:T(512)(128)(4,1)}, u32[]{:S(2)}) copy-start(pred[512]{0:T(512)(128)(4,1)} %constant.73.clone.1) | copy-start | bytes 1540
  109.6 14.3 %copy-start.1 = (bf16[8,256,512]{2,1,0:T(8,128)(2,1)S(1)}, bf16[8,256,512]{2,1,0:T(8,128)(2,1)}, u32[]{:S(2)}) copy-start(bf16[8,256,512]{2,1,0:T(8,128)(2,1)} %get-tuple-element.35) | copy-start | bytes 6291460
  109.6 14.3 %collective-permute-start.7 = (bf16[8,256,512]{2,1,0:T(8,128)(2,1)}, bf16[8,256,512]{2,1,0:T(8,128)(2,1)}, u32[]{:S(2)}, u32[]{:S(2)}) collective-permute-start(bf16[8,256,512]{2,1,0:T(8,128)(2,1)} %get-tuple-element.35), channel_id=1, source_target_pairs={{0,1},{1,0},{2,3},{3,2},{4,5},{5,4},{6,7},{7,6},{8,9},{9,8},{10,11... | collective-permute-start | bytes 6291464 | tf_op jit(solution)/shard_map/ppermute | solution.py:329
  111.0 2.9 %collective-permute-start.9 = (f32[15,512]{1,0:T(8,128)S(1)}, f32[15,512]{1,0:T(8,128)S(1)}, u32[]{:S(2)}, u32[]{:S(2)}) collective-permute-start(f32[15,512]{1,0:T(8,128)S(1)} %pad_maximum_fusion.3), channel_id=1, source_target_pairs={{0,1},{1,0},{2,3},{3,2},{4,5},{5,4},{6,7},{7,6},{8,9},{9,8},{10,11... | collective-permute-start | bytes 92168 | tf_op jit(solution)/shard_map/ppermute | solution.py:329
  111.4 17.9 %collective-permute-start.6 = (bf16[8,256,512]{2,1,0:T(8,128)(2,1)}, bf16[8,256,512]{2,1,0:T(8,128)(2,1)}, u32[]{:S(2)}, u32[]{:S(2)}) collective-permute-start(bf16[8,256,512]{2,1,0:T(8,128)(2,1)} %get-tuple-element.34), channel_id=1, source_target_pairs={{0,1},{1,0},{2,3},{3,2},{4,5},{5,4},{6,7},{7,6},{8,9},{9,8},{10,11... | collective-permute-start | bytes 6291464 | tf_op jit(solution)/shard_map/ppermute | solution.py:329
  115.2 34.7 %all-to-all-start.1 = ((bf16[8,512,128]{2,1,0:T(8,128)(2,1)}), bf16[8,512,128]{2,1,0:T(8,128)(2,1)S(1)}, u32[]{:S(2)}, u32[]{:S(2)}) async-start(bf16[8,512,128]{2,1,0:T(8,128)(2,1)} %broadcast_in_dim.39), calls=%async_computation.1 | async-start | bytes 2097152 | tf_op jit(solution)/shard_map/all_to_all | solution.py:333
  123.9 5.5 %copy-start.2 = (bf16[8,256,512]{2,1,0:T(8,128)(2,1)S(1)}, bf16[8,256,512]{2,1,0:T(8,128)(2,1)}, u32[]{:S(2)}) copy-start(bf16[8,256,512]{2,1,0:T(8,128)(2,1)} %get-tuple-element.34) | copy-start | bytes 6291460

commit v2 on v0

v2 whole, which is shorter than its diff:
```python
import functools

import jax
import jax.numpy as jnp
from jax import lax
from jax.experimental import pallas as pl
from jax.experimental.pallas import tpu as pltpu
from jax.sharding import PartitionSpec as P

EPS = 1e-06
BF, F32 = jnp.bfloat16, jnp.float32
TILE = 256
LANES = 128
PAD = 8
CHUNK = 64
VMEM_LIMIT = 60 * 1024 * 1024


def params():
    return pltpu.CompilerParams(dimension_semantics=("arbitrary",), vmem_limit_bytes=VMEM_LIMIT)


def struct(shape, dtype):
    return jax.ShapeDtypeStruct(shape, dtype)


def whole(shape):
    return pl.BlockSpec(shape, lambda *_: (0,) * len(shape))


def any_spec():
    return pl.BlockSpec(memory_space=pl.ANY)


def lane(q):
    return slice(q * LANES, (q + 1) * LANES)


def fold(x):
    return jnp.sum(x.reshape(x.shape[0] // 8, 8, x.shape[1]), axis=0)


def pick(table, group):
    rows = table[...].astype(F32)
    value = rows[0:1]
    for r in range(1, rows.shape[0]):
        value = jnp.where(group == r, rows[r:r + 1], value)
    return value


def as_row(ref):
    return ref[...].astype(F32).reshape(1, -1)


def gelu_parts(pre):
    cdf = 0.5 + 0.5 * lax.erf(pre * 0.7071067811865476)
    density = jnp.exp(-0.5 * pre * pre) * 0.3989422804014327
    return pre * cdf, cdf + pre * density


def dot(a, b):
    return jnp.dot(a, b, preferred_element_type=F32)


def dot_t(a, b):
    return lax.dot_general(a, b, (((1,), (1,)), ((), ())), preferred_element_type=F32)


def dot_rows(a, b):
    return lax.dot_general(a, b, (((0,), (0,)), ((), ())), preferred_element_type=F32)


def place_items(n, core, counts, offs):
    end = jnp.int32(0)
    for j in range(n):
        offs[j] = end
        end = end + (counts[core[0] * n + j] + 15) // 16 * 16
    offs[n] = end
    offs[n + 1] = (end + TILE - 1) // TILE


def pack_kernel(wi, bi, wo, out):
    width, h = wi.shape
    hq, wq = h // LANES, width // LANES
    for q in range(hq):
        out[q * width:(q + 1) * width, :] = wi[:, lane(q)]
    base = hq * width
    for q in range(wq):
        out[base + q * h:base + (q + 1) * h, :] = wo[:, lane(q)]
    base += wq * h
    bias = bi[...].astype(F32).reshape(1, h)
    rows = [bias[:, lane(q)] for q in range(hq)] + [jnp.zeros((1, LANES), F32)] * (16 - hq)
    out[base:base + 16, :] = jnp.concatenate(rows, axis=0).astype(BF)


def pack(wi, bi, wo):
    rows = 2 * wi.size // LANES + 16
    return pl.pallas_call(pack_kernel, out_shape=struct((rows, LANES), BF),
                          compiler_params=pltpu.CompilerParams(vmem_limit_bytes=VMEM_LIMIT))(wi, bi, wo)


def weight_copies(buf, side, win, wout, bias, sems):
    width, h = win.shape[0], win.shape[1] // 2
    hq, wq = h // LANES, width // LANES
    copies = []
    for q in range(hq):
        at = side * h + q * LANES
        copies.append((buf.at[pl.ds(q * width, width), :], win.at[:, pl.ds(at, LANES)]))
    base = hq * width
    for q in range(wq):
        copies.append((buf.at[pl.ds(base + q * h, h), :], wout.at[pl.ds(side * h, h), pl.ds(q * LANES, LANES)]))
    copies.append((buf.at[pl.ds(base + wq * h, 16), :], bias.at[side]))
    return [pltpu.make_async_copy(src, dst, sems.at[side, i]) for i, (src, dst) in enumerate(copies)]


def spread_bias(bias, row):
    hq = row.shape[1] // LANES // 2
    for side in range(2):
        for q in range(hq):
            at = side * hq + q
            row[:, lane(at)] = bias[side, q:q + 1, :].astype(F32)


def front_kernel(n, core, counts, groups, tok, cot, cw, cb, ns, nsh, gamma, buf_a, buf_b,
                 ad_o, nrm_o, low_o, inv_o, act_o, pre_o, keep, send, gbo, gbi,
                 offs, pad, ad, nrm, low, inv, win, wout, bias, bias_row, dwo, dwi, sems):
    s = pl.program_id(0)
    frames, width = tok.shape[1], tok.shape[2]
    taps = cw.shape[0]
    half = taps // 2
    wq = width // LANES
    h = win.shape[1] // 2
    copies = weight_copies(buf_a, 0, win, wout, bias, sems) + weight_copies(buf_b, 1, win, wout, bias, sems)

    @pl.when(s == 0)
    def _():
        for c in copies:
            c.start()
        place_items(n, core, counts, offs)
        gbo[...] = jnp.zeros_like(gbo)
        pad[...] = jnp.zeros_like(pad)

    @pl.when(s < n)
    def _():
        item = core[0] * n + s
        count = counts[item]
        group = groups[item]
        off = offs[s]
        rows = lax.broadcasted_iota(jnp.int32, (frames, 1), 0)
        for q in range(wq):
            pad[q, PAD:PAD + frames, :] = jnp.where(rows < count, tok[0, :, lane(q)].astype(F32), 0.0)
        scale, shift = pick(ns, group), pick(nsh, group)
        gam, conv_bias = as_row(gamma), as_row(cb)
        w = cw[...].astype(F32)

        def step(i, acc):
            r0 = pl.multiple_of(i * CHUNK, CHUNK)
            live = (lax.broadcasted_iota(jnp.int32, (CHUNK, 1), 0) + r0) < count
            convs = []
            for q in range(wq):
                conv = conv_bias[:, lane(q)]
                for k in range(taps):
                    conv = conv + w[k:k + 1, lane(q)] * pad[q, pl.ds(r0 + (PAD - half + k), CHUNK), :]
                convs.append(conv)
            mean = jnp.sum(sum(convs[1:], convs[0]), axis=-1, keepdims=True) * (1.0 / width)
            cents = [c - mean for c in convs]
            sq = [c * c for c in cents]
            var = jnp.sum(sum(sq[1:], sq[0]), axis=-1, keepdims=True) * (1.0 / width)
            istd = lax.rsqrt(var + EPS)
            dst = pl.ds(pl.multiple_of(off + r0, 16), CHUNK)
            inv[dst, :] = jnp.broadcast_to(istd, (CHUNK, LANES))
            new = []
            for q in range(wq):
                normed = cents[q] * istd
                ad[dst, lane(q)] = (normed * scale[:, lane(q)] + shift[:, lane(q)]).astype(BF)
                nrm[dst, lane(q)] = normed.astype(BF)
                back = jnp.where(live, cot[0, pl.ds(r0, CHUNK), lane(q)].astype(F32), 0.0) * gam[:, lane(q)]
                low[dst, lane(q)] = back.astype(BF)
                new.append(acc[q] + fold(back))
            return tuple(new)

        accs = lax.fori_loop(0, pl.cdiv(count, CHUNK), step, (jnp.zeros((8, LANES), F32),) * wq)
        for q in range(wq):
            gbo[:, lane(q)] += accs[q]

    @pl.when(s == n)
    def _():
        end = pl.ds(pl.multiple_of(offs[n], 16), TILE)
        ad[end, :] = jnp.zeros((TILE, width), BF)
        low[end, :] = jnp.zeros((TILE, width), BF)
        for c in copies:
            c.wait()
        spread_bias(bias, bias_row)
        dwo[...] = jnp.zeros_like(dwo)
        dwi[...] = jnp.zeros_like(dwi)
        gbi[...] = jnp.zeros_like(gbi)

    @pl.when((s >= n) & (s - n < offs[n + 1]))
    def _():
        at = pl.ds(pl.multiple_of((s - n) * TILE, TILE), TILE)
        a, b = ad[at, :], low[at, :]
        ad_o[...] = a
        low_o[...] = b
        nrm_o[...] = nrm[at, :]
        inv_o[...] = inv[at, :]
        activation, slope = gelu_parts(dot(a, win[...]) + bias_row[...])
        grad = dot_t(b, wout[...]) * slope
        lo = activation.astype(BF)
        act_o[...] = lo
        dwo[...] += dot_rows(lo, b)
        gbi[...] += fold(grad)
        g = grad.astype(BF)
        pre_o[...] = g
        dwi[...] += dot_rows(a, g)

    @pl.when(s == pl.num_programs(0) - 1)
    def _():
        for side, dst in ((0, keep), (1, send)):
            for q in range(wq):
                dst[q * h:(q + 1) * h, :] = dwo[side * h:(side + 1) * h, lane(q)].astype(dst.dtype)
            base = wq * h
            for q in range(h // LANES):
                dst[base + q * width:base + (q + 1) * width, :] = dwi[:, lane(side * (h // LANES) + q)].astype(dst.dtype)


def front(core, counts, groups, tok, cot, cw, cb, ns, nsh, gamma, buf_a, buf_b, h):
    items, frames, width = tok.shape
    n = items // 2
    tiles = n * frames // TILE
    rows = n * frames + TILE
    packed = 2 * width * h // LANES
    wq, hq = width // LANES, h // LANES
    item = pl.BlockSpec((1, frames, width), lambda s, c, *_: (c[0] * n + jnp.minimum(s, n - 1), 0, 0))

    def tiled(cols):
        return pl.BlockSpec((TILE, cols), lambda s, *_: (jnp.maximum(s - n, 0), 0))

    return pl.pallas_call(
        functools.partial(front_kernel, n),
        grid_spec=pltpu.PrefetchScalarGridSpec(
            num_scalar_prefetch=3, grid=(n + tiles,),
            in_specs=[item, item] + [whole(v.shape) for v in (cw, cb, ns, nsh, gamma)] + [any_spec()] * 2,
            out_specs=[tiled(width), tiled(width), tiled(width), tiled(LANES), tiled(2 * h), tiled(2 * h),
                       whole((packed, LANES)), whole((packed, LANES)), whole((8, width)), whole((8, 2 * h))],
            scratch_shapes=[pltpu.SMEM((n + 2,), jnp.int32),
                            pltpu.VMEM((wq, frames + 4 * PAD, LANES), F32),
                            pltpu.VMEM((rows, width), BF), pltpu.VMEM((rows, width), BF),
                            pltpu.VMEM((rows, width), BF), pltpu.VMEM((rows, LANES), F32),
                            pltpu.VMEM((width, 2 * h), BF), pltpu.VMEM((2 * h, width), BF),
                            pltpu.VMEM((2, 16, LANES), BF), pltpu.VMEM((1, 2 * h), F32),
                            pltpu.VMEM((2 * h, width), F32), pltpu.VMEM((width, 2 * h), F32),
                            pltpu.SemaphoreType.DMA((2, hq + wq + 1))]),
        out_shape=[struct((tiles * TILE, width), BF)] * 3 + [struct((tiles * TILE, LANES), F32)]
        + [struct((tiles * TILE, 2 * h), BF)] * 2
        + [struct((packed, LANES), F32), struct((packed, LANES), BF), struct((8, width), F32), struct((8, 2 * h), F32)],
        compiler_params=params(),
    )(core, counts, groups, tok, cot, cw, cb, ns, nsh, gamma, buf_a, buf_b)


def back_kernel(n, tiles, core, counts, groups, tok, cot, ad_i, nrm_i, low_i, inv_i, act_i, pre_i, gbo, gbi,
                cw, ns, gamma, bout, buf_a, buf_b, buf_c, buf_d,
                out, gtok, out_t, gtok_t, small_keep, small_send,
                offs, win1, wout1, win2, wout2, bias, bias_row, nrm, inv, branch, ag, cgp, sums, sems):
    s = pl.program_id(0)
    frames, width = tok.shape[1], tok.shape[2]
    taps, rates = cw.shape[0], ns.shape[0]
    half = taps // 2
    wq = width // LANES
    h = win1.shape[1] // 2
    copies = (weight_copies(buf_a, 0, win1, wout1, bias, sems.at[0]) + weight_copies(buf_b, 1, win1, wout1, bias, sems.at[0]))
    copies2 = (weight_copies(buf_c, 0, win2, wout2, bias, sems.at[1]) + weight_copies(buf_d, 1, win2, wout2, bias, sems.at[1]))
    biases = (wq + h // LANES, 2 * (wq + h // LANES) + 1)

    @pl.when(s == 0)
    def _():
        for c in copies2:
            c.start()
        for i, c in enumerate(copies):
            if i not in biases:
                c.start()
        place_items(n, core, counts, offs)
        sums[...] = jnp.zeros_like(sums)
        cgp[...] = jnp.zeros_like(cgp)
        for c in copies2:
            c.wait()
        spread_bias(bias, bias_row)
        for i, c in enumerate(copies):
            if i not in biases:
                c.wait()

    @pl.when((s < tiles) & (s < offs[n + 1]))
    def _():
        at = pl.ds(pl.multiple_of(s * TILE, TILE), TILE)
        a, b = ad_i[...], low_i[...]
        nrm[at, :] = nrm_i[...]
        inv[at, :] = inv_i[...]
        activation, slope = gelu_parts(dot(a, win2[...]) + bias_row[...])
        grad = dot_t(b, wout2[...]) * slope
        branch[at, :] = (dot(act_i[...], wout1[...]) + dot(activation.astype(BF), wout2[...])) + as_row(bout)
        ag[at, :] = dot_t(pre_i[...], win1[...]) + dot_t(grad.astype(BF), win2[...])

    @pl.when(s >= tiles)
    def _():
        j = s - tiles
        item = core[0] * n + j
        count = counts[item]
        group = groups[item]
        off = offs[j]
        scale = pick(ns, group)
        gam = as_row(gamma)
        w = cw[...].astype(F32)
        zero = jnp.zeros((8, LANES), F32)
        steps = pl.cdiv(count, CHUNK)

        def step(i, accs):
            r0 = pl.multiple_of(i * CHUNK, CHUNK)
            here = pl.ds(r0, CHUNK)
            live = (lax.broadcasted_iota(jnp.int32, (CHUNK, 1), 0) + r0) < count
            src = pl.ds(pl.multiple_of(off + r0, 16), CHUNK)
            new = []
            ngs, nrs = [], []
            for q in range(wq):
                a_ls, a_sc, a_sh = accs[3 * q:3 * q + 3]
                br = jnp.where(live, branch[src, lane(q)], 0.0)
                tk = jnp.where(live, tok[0, here, lane(q)].astype(F32), 0.0)
                o = (tk + gam[:, lane(q)] * br).astype(BF)
                out[0, here, lane(q)] = o
                out_t[0, here, lane(q)] = o
                g = jnp.where(live, ag[src, lane(q)], 0.0)
                nr = nrm[src, lane(q)].astype(F32)
                new += [a_ls + fold(cot[0, here, lane(q)].astype(F32) * br), a_sc + fold(g * nr), a_sh + fold(g)]
                ngs.append(g * scale[:, lane(q)])
                nrs.append(nr)
            cross = [a * b for a, b in zip(ngs, nrs)]
            m1 = jnp.sum(sum(ngs[1:], ngs[0]), axis=-1, keepdims=True) * (1.0 / width)
            m2 = jnp.sum(sum(cross[1:], cross[0]), axis=-1, keepdims=True) * (1.0 / width)
            istd = inv[src, :]
            for q in range(wq):
                cg = istd * (ngs[q] - m1 - nrs[q] * m2)
                cgp[q, pl.ds(pl.multiple_of(r0 + PAD, 8), CHUNK), :] = jnp.where(live, cg, 0.0)
            return tuple(new)

        accs = lax.fori_loop(0, steps, step, (zero,) * (3 * wq))
        for q in range(wq):
            sums[taps + 1, :, lane(q)] += accs[3 * q]
            sums[taps + 2 + group, :, lane(q)] += accs[3 * q + 1]
            sums[taps + 2 + rates + group, :, lane(q)] += accs[3 * q + 2]

        def clear(i, _):
            r0 = pl.multiple_of(i * CHUNK, CHUNK)
            here = pl.ds(r0, CHUNK)
            out[0, here, :] = jnp.zeros((CHUNK, width), BF)
            out_t[0, here, :] = jnp.zeros((CHUNK, width), BF)
            gtok[0, here, :] = jnp.zeros((CHUNK, width), F32)
            gtok_t[0, here, :] = jnp.zeros((CHUNK, width), BF)
            for q in range(wq):
                cgp[q, pl.ds(pl.multiple_of(r0 + PAD, 8), CHUNK), :] = jnp.zeros((CHUNK, LANES), F32)
            return 0

        lax.fori_loop(steps, frames // CHUNK, clear, 0)

        for q in range(wq):
            wl = w[:, lane(q)]

            def conv_step(i, accs):
                r0 = pl.multiple_of(i * CHUNK, CHUNK)
                here = pl.ds(r0, CHUNK)
                live = (lax.broadcasted_iota(jnp.int32, (CHUNK, 1), 0) + r0) < count
                tk = jnp.where(live, tok[0, here, lane(q)].astype(F32), 0.0)
                total = cot[0, here, lane(q)].astype(F32)
                new = []
                for k in range(taps):
                    sh = cgp[q, pl.ds(r0 + (PAD + half - k), CHUNK), :]
                    total = total + wl[k:k + 1] * sh
                    new.append(accs[k] + fold(tk * sh))
                    if k == half:
                        new_bias = accs[taps] + fold(sh)
                total = jnp.where(live, total, 0.0).astype(BF)
                gtok_t[0, here, lane(q)] = total
                gtok[0, here, lane(q)] = total.astype(F32)
                return tuple(new) + (new_bias,)

            accs = lax.fori_loop(0, steps, conv_step, (zero,) * (taps + 1))
            for k in range(taps + 1):
                sums[k, :, lane(q)] += accs[k]

    @pl.when(s == pl.num_programs(0) - 1)
    def _():
        last = taps + 2 + 2 * rates
        rows = [jnp.sum(sums[i], axis=0, keepdims=True) for i in range(last)]
        rows.append(jnp.sum(gbo[...], axis=0, keepdims=True))
        gb = jnp.sum(gbi[...], axis=0, keepdims=True)
        fill = jnp.zeros((1, width - h), F32)
        spare = [jnp.zeros((1, width), F32)] * (small_keep.shape[0] - last - 2)
        for side, dst in ((0, small_keep), (1, small_send)):
            tail = [jnp.concatenate([gb[:, side * h:(side + 1) * h], fill], axis=1)]
            dst[...] = jnp.concatenate(rows + tail + spare, axis=0)


def back(core, counts, groups, tok, cot, ad, nrm, low, inv, act, pre, gbo, gbi, cw, ns, gamma, bout, bufs):
    items, frames, width = tok.shape
    n = items // 2
    h = act.shape[1] // 2
    tiles = n * frames // TILE
    rows = n * frames + TILE
    wq, hq = width // LANES, h // LANES
    taps, rates = cw.shape[0], ns.shape[0]
    n_small = -(-(taps + 4 + 2 * rates) // 8) * 8

    def at(s):
        return jnp.maximum(s - tiles, 0)

    item = pl.BlockSpec((1, frames, width), lambda s, c, *_: (c[0] * n + at(s), 0, 0))
    mine = pl.BlockSpec((1, frames, width), lambda s, *_: (at(s), 0, 0))

    def tiled(cols):
        return pl.BlockSpec((TILE, cols), lambda s, *_: (jnp.minimum(s, tiles - 1), 0))

    return pl.pallas_call(
        functools.partial(back_kernel, n, tiles),
        grid_spec=pltpu.PrefetchScalarGridSpec(
            num_scalar_prefetch=3, grid=(tiles + n,),
            in_specs=[item, item, tiled(width), tiled(width), tiled(width), tiled(LANES), tiled(2 * h), tiled(2 * h)]
            + [whole(v.shape) for v in (gbo, gbi, cw, ns, gamma, bout)] + [any_spec()] * 4,
            out_specs=[item, item, mine, mine, whole((n_small, width)), whole((n_small, width))],
            scratch_shapes=[pltpu.SMEM((n + 2,), jnp.int32),
                            pltpu.VMEM((width, 2 * h), BF), pltpu.VMEM((2 * h, width), BF),
                            pltpu.VMEM((width, 2 * h), BF), pltpu.VMEM((2 * h, width), BF),
                            pltpu.VMEM((2, 16, LANES), BF), pltpu.VMEM((1, 2 * h), F32),
                            pltpu.VMEM((rows, width), BF), pltpu.VMEM((rows, LANES), F32),
                            pltpu.VMEM((rows, width), F32), pltpu.VMEM((rows, width), F32),
                            pltpu.VMEM((wq, frames + 4 * PAD, LANES), F32),
                            pltpu.VMEM((taps + 2 + 2 * rates, 8, width), F32),
                            pltpu.SemaphoreType.DMA((2, 2, hq + wq + 1))]),
        out_shape=[struct((items, frames, width), BF), struct((items, frames, width), F32),
                   struct((n, frames, width), BF), struct((n, frames, width), BF),
                   struct((n_small, width), F32), struct((n_small, width), F32)],
        compiler_params=params(),
    )(core, counts, groups, tok, cot, ad, nrm, low, inv, act, pre, gbo, gbi, cw, ns, gamma, bout, *bufs)


def merge_kernel(core, out_b, gtok_b, out_in, gtok_in, out, gtok):
    out[...] = out_b[...]
    gtok[...] = gtok_b[...].astype(F32)


def merge(core, out_b, gtok_b, out, gtok):
    n, frames, width = out_b.shape
    mine = pl.BlockSpec((1, frames, width), lambda s, c: (s, 0, 0))
    other = pl.BlockSpec((1, frames, width), lambda s, c: ((1 - c[0]) * n + s, 0, 0))
    return pl.pallas_call(
        merge_kernel,
        grid_spec=pltpu.PrefetchScalarGridSpec(
            num_scalar_prefetch=1, grid=(n,),
            in_specs=[mine, mine, any_spec(), any_spec()], out_specs=[other, other]),
        out_shape=[struct(out.shape, out.dtype), struct(gtok.shape, gtok.dtype)],
        input_output_aliases={3: 0, 4: 1},
        compiler_params=params(),
    )(core, out_b, gtok_b, out, gtok)


def message_kernel(shard, keep, recv, out, total):
    total_rows = shard.shape[1]
    acc = shard[0].astype(F32)
    for i in range(1, shard.shape[0]):
        acc = acc + shard[i].astype(F32)
    total[:total_rows, :] = acc.astype(BF)
    small = keep[...] + recv[...]
    high = small.astype(BF)
    low = (small - high.astype(F32)).astype(BF)
    n_small = small.shape[0]
    wq = small.shape[1] // LANES
    for part, value in enumerate((high, low)):
        for q in range(wq):
            base = total_rows + (part * wq + q) * n_small
            total[base:base + n_small, :] = value[:, lane(q)]
    for i in range(out.shape[0]):
        out[i] = total[...]


def make_message(shard, keep, recv):
    dp, m, _ = shard.shape
    rows = m + 2 * keep.size // LANES
    return pl.pallas_call(
        message_kernel, out_shape=struct((dp, rows, LANES), BF),
        scratch_shapes=[pltpu.VMEM((rows, LANES), BF)],
        compiler_params=pltpu.CompilerParams(vmem_limit_bytes=VMEM_LIMIT))(shard, keep, recv)


def unpack_kernel(m, taps, rates, msg, gcw, gcb, gns, gnsh, gwi, gbi, gwo, gbo, gls, full):
    dp = msg.shape[0]
    h, width = gwo.shape
    wq, hq = width // LANES, h // LANES
    for i in range(dp):
        full[i * m:(i + 1) * m, :] = msg[i, :m, :].astype(F32)
    for q in range(wq):
        gwo[:, lane(q)] = full[q * h:(q + 1) * h, :]
    base = wq * h
    for q in range(hq):
        gwi[:, lane(q)] = full[base + q * width:base + (q + 1) * width, :]
    both = msg[0, m:, :].astype(F32)
    for i in range(1, dp):
        both = both + msg[i, m:, :].astype(F32)
    k = both.shape[0] // 2
    small = both[:k] + both[k:]
    rows = k // wq
    small = jnp.concatenate([small[q * rows:(q + 1) * rows] for q in range(wq)], axis=1)
    gcw[...] = small[:taps]
    gcb[...] = small[taps:taps + 1]
    gls[...] = small[taps + 1:taps + 2]
    gns[...] = small[taps + 2:taps + 2 + rates]
    gnsh[...] = small[taps + 2 + rates:taps + 2 + 2 * rates]
    at = taps + 2 + 2 * rates
    gbo[...] = small[at:at + 1]
    gbi[...] = small[at + 1:at + 2, :h]


def unpack(msg, m, taps, rates, width, h):
    shapes = [(taps, width), (1, width), (rates, width), (rates, width), (width, h), (1, h), (h, width), (1, width), (1, width)]
    return pl.pallas_call(
        functools.partial(unpack_kernel, m, taps, rates), out_shape=[struct(s, F32) for s in shapes],
        scratch_shapes=[pltpu.VMEM((msg.shape[0] * m, LANES), F32)],
        compiler_params=pltpu.CompilerParams(vmem_limit_bytes=VMEM_LIMIT))(msg)


def swap(x, step):
    size = lax.axis_size("tp")
    return lax.ppermute(x, "tp", [(i, i ^ step) for i in range(size)])


def exchange(x):
    return lax.all_to_all(x, "dp", 0, 0)


def per_device(tokens, frame_counts, rate_groups, conv_weight, conv_bias, norm_scale, norm_shift,
               weight_in, bias_in, weight_out, bias_out, layer_scale, cotangent):
    width, h = weight_in.shape
    taps, rates = conv_weight.shape[0], norm_scale.shape[0]
    dp = lax.axis_size("dp")
    core = (lax.axis_index("tp") % 2).astype(jnp.int32).reshape(1)

    buf_a = pack(weight_in, bias_in, weight_out)
    buf_b = swap(buf_a, 1)
    buf_c = swap(buf_a, 2)
    buf_d = swap(buf_c, 1)
    ad, nrm, low, inv, act, pre, keep, send, gbo, gbi = front(
        core, frame_counts, rate_groups, tokens, cotangent, conv_weight, conv_bias, norm_scale, norm_shift,
        layer_scale, buf_a, buf_b, h)
    grads = (keep + swap(send, 1).astype(F32)).astype(BF)
    shard = exchange(grads.reshape(dp, grads.shape[0] // dp, LANES))
    out, gtok, out_t, gtok_t, small_keep, small_send = back(
        core, frame_counts, rate_groups, tokens, cotangent, ad, nrm, low, inv, act, pre, gbo, gbi,
        conv_weight, norm_scale, layer_scale, bias_out, (buf_a, buf_b, buf_c, buf_d))
    message = exchange(make_message(shard, small_keep, swap(small_send, 1)))
    out, gtok = merge(core, swap(out_t, 1), swap(gtok_t, 1), out, gtok)
    gcw, gcb, gns, gnsh, gwi, gbi, gwo, gbo, gls = unpack(message, shard.shape[1], taps, rates, width, h)
    flat = lambda v: v.reshape(-1)
    return (out, gtok, gcw, flat(gcb), gns, gnsh, gwi, flat(gbi), gwo, flat(gbo), flat(gls))


def solution(mesh):
    items, copied = P("dp", None, None), P()
    in_specs = (items, P("dp"), P("dp"), copied, copied, copied, copied, P(None, "tp"), P("tp"), P("tp", None),
                copied, copied, items)
    out_specs = (items, items, copied, copied, copied, copied, P(None, "tp"), P("tp"), P("tp", None), copied, copied)
    return jax.shard_map(per_device, mesh=mesh, in_specs=in_specs, out_specs=out_specs, check_vma=False)
```

time: 497 us -> 128 us (0.26)
  waiting for transfers between devices: 282 us -> 35.6 us
  other arithmetic: 100 us -> 3.75 us
  Pallas kernels: 0 us -> 62.7 us
  matrix products: 55.2 us -> 0 us
  blocking collectives: 37.7 us -> 0 us
  starting transfers between devices: 0.26 us -> 21.2 us
  between operations: 14.7 us -> 0.69 us
    psum x2 -> x0, waiting for transfers between devices: 282 us -> none  [the longest x1 282 us: per_device(): lax.psum(jnp.dot(act_low, weight_out, preferred_element_type=jnp.float32)...]
    reduce_sum x4 -> x0, other arithmetic: 93.1 us -> none  [the longest x1 37.2 us: per_device(): grad_gamma = jnp.sum(grad_rows * branch, axis=0)]
    pallas_call x0 -> x6, Pallas kernels: none -> 62.7 us  [the longest x1 28 us: back(): pl.pallas_call(functools.partial(back_kernel, n, tiles), grid_spec=pltpu....]
    dot_general x11 -> x0, matrix products: 55.2 us -> none  [the longest x4 24.5 us: contract_rows(): lax.dot_general(left, right, (((0,), (0,)), ((), ())), precision=precisio...]
    psum x1 -> x0, blocking collectives: 37.7 us -> none  [per_device(): lax.psum((grad_weight_in, grad_bias_in, grad_weight_out, grad_conv_weight...]
    all_to_all x0 -> x2, waiting for transfers between devices: none -> 19.2 us  [exchange(): return lax.all_to_all(x, 'dp', 0, 0)]
    ppermute x0 -> x7, waiting for transfers between devices: none -> 16.4 us  [swap(): return lax.ppermute(x, 'tp', [(i, i ^ step) for i in range(size)])]
    all_to_all x0 -> x2, starting transfers between devices: none -> 16 us  [exchange(): return lax.all_to_all(x, 'dp', 0, 0)]
  transfers between devices with their start and end apart: 2 -> 9, of which waited for: 1 -> 5; matrix products, arithmetic and copies ran while one was open for 21% -> 2% of each run, Pallas kernels for 0% -> 29%
where the time goes in v2:
time: 128 us
  Pallas kernels  62.7 us (49%)
  waiting for transfers between devices  35.6 us (28%)
  starting transfers between devices  21.2 us (17%)
  other arithmetic  3.75 us (3%)
  local copies, waits for them, and re-layouts  3.66 us (3%)
    pallas_call x1, Pallas kernels, back(): pl.pallas_call(functools.partial(back_kernel, n, tiles), grid_spec=pltpu....  28 us
    pallas_call x1, Pallas kernels, front(): pl.pallas_call(functools.partial(front_kernel, n), grid_spec=pltpu.Prefet...  20.8 us
    all_to_all x2, waiting for transfers between devices, exchange(): return lax.all_to_all(x, 'dp', 0, 0)  19.2 us
    ppermute x7, waiting for transfers between devices, swap(): return lax.ppermute(x, 'tp', [(i, i ^ step) for i in range(size)])  16.4 us
    all_to_all x2, starting transfers between devices, exchange(): return lax.all_to_all(x, 'dp', 0, 0)  16 us
    pallas_call x1, Pallas kernels, merge(): pl.pallas_call(merge_kernel, grid_spec=pltpu.PrefetchScalarGridSpec(num_s...  6.87 us
    ppermute x7, starting transfers between devices, swap(): return lax.ppermute(x, 'tp', [(i, i ^ step) for i in range(size)])  5.18 us
    unnamed x14, local copies, waits for them, and re-layouts  3.66 us
  transfers between devices with their start and end apart: 9, of which 5 were waited for; matrix products, arithmetic and copies ran while one was open for 2% of the time, Pallas kernels for 29%

profile of v2, /device:TPU:0, one launch (start us, length us, event | category | flops | bytes accessed | tf_op | source)
XLA Modules:
  0.0 127.6 jit_solution(28544790181003026)
XLA Ops:
  0.6 2.2 %shard_map.212.buf_a = bf16[3088,128]{1,0:T(8,128)(2,1)} custom-call(bf16[512,384]{1,0:T(8,128)(2,1)} %wi.1, bf16[384]{0:T(512)(128)(2,1)} %bi.1, bf16[384,512]{1,0:T(8,128)(2,1)} %wo.1), custom_call_target="tpu_custom_call" | custom-call | tf_op jit(solution)/shard_map/pallas_call | solution.py:98
  2.8 0.5 collective-permute-start
  3.3 2.1 %collective-permute-done.buf_b = bf16[3088,128]{1,0:T(8,128)(2,1)S(1)} collective-permute-done((bf16[3088,128]{1,0:T(8,128)(2,1)}, bf16[3088,128]{1,0:T(8,128)(2,1)S(1)}, u32[]{:S(2)}, u32[]{:S(2)}) %collective-permute-start) | collective-permute-done | bytes 790560 | tf_op jit(solution)/shard_map/ppermute | solution.py:528
  5.4 0.0 copy-start.2
  5.4 0.9 copy-done.2
  6.3 0.0 copy-start
  6.3 20.8 %shard_map.213 = (bf16[2048,512]{1,0:T(8,128)(2,1)}, bf16[2048,512]{1,0:T(8,128)(2,1)}, bf16[2048,512]{1,0:T(8,128)(2,1)}, f32[2048,128]{1,0:T(8,128)}, bf16[204...) custom-call(s32[1]{0:T(128)} %bitcast.core, ...), custom_call_target="tpu_custom_call" | custom-call | tf_op jit(solution)/shard_map/pallas_call | solution.py:238
  27.1 0.8 collective-permute-start.5
  27.9 0.0 copy-done
  27.9 2.6 %collective-permute-start.1 = (bf16[3088,128]{1,0:T(8,128)(2,1)S(1)}, bf16[3088,128]{1,0:T(8,128)(2,1)S(1)}, u32[]{:S(2)}, u32[]{:S(2)}) collective-permute-start(bf16[3088,128]{1,0:T(8,128)(2,1)S(1)} %copy-done), channel_id=1, source_target_pairs={{0,2},{1,3},{2,0},{3,1},{4,6},{5,7},{6,4},{7,5},{8,10},{9,11},{10,... | collective-permute-start | bytes 2371592 | tf_op jit(solution)/shard_map/ppermute | solution.py:528
  30.5 0.0 collective-permute-done.5
  30.5 2.5 %add_convert_fusion = bf16[3072,128]{1,0:T(8,128)(2,1)} fusion(f32[3072,128]{1,0:T(8,128)} %get-tuple-element.52, bf16[3072,128]{1,0:T(8,128)(2,1)S(1)} %collective-permute-done.5), kind=kLoop, calls=%fused_computation | loop fusion | flops 1179648 | bytes 3145728 | tf_op jit(solution)/shard_map/convert_element_type | solution.py:549
  33.0 7.0 %all-to-all-start = ((bf16[8,384,128]{2,1,0:T(8,128)(2,1)}), bf16[8,384,128]{2,1,0:T(8,128)(2,1)S(1)}, u32[]{:S(2)}, u32[]{:S(2)}) async-start(bf16[8,384,128]{2,1,0:T(8,128)(2,1)} %bitcast.1), calls=%async_computation | async-start | bytes 1572864 | tf_op jit(solution)/shard_map/all_to_all | solution.py:532
  40.0 8.4 %collective-permute-done.1.buf_c = bf16[3088,128]{1,0:T(8,128)(2,1)S(1)} collective-permute-done((bf16[3088,128]{1,0:T(8,128)(2,1)S(1)}, bf16[3088,128]{1,0:T(8,128)(2,1)S(1)}, u32[]{:S(2)}, u32[]{:S(2)}) %collective-permute-start.1) | collective-permute-done | bytes 790560 | tf_op jit(solution)/shard_map/ppermute | solution.py:528
  48.4 0.0 copy-start.4
  48.4 0.0 collective-permute-start.2
  48.4 2.3 %collective-permute-done.2.buf_d = bf16[3088,128]{1,0:T(8,128)(2,1)S(1)} collective-permute-done((bf16[3088,128]{1,0:T(8,128)(2,1)S(1)}, bf16[3088,128]{1,0:T(8,128)(2,1)S(1)}, u32[]{:S(2)}, u32[]{:S(2)}) %collective-permute-start.2) | collective-permute-done | bytes 790560 | tf_op jit(solution)/shard_map/ppermute | solution.py:528
  50.7 0.0 copy-start.5
  50.7 0.0 copy-done.4
  50.7 0.9 copy-done.5
  51.6 28.0 %shard_map.214 = (bf16[16,256,512]{2,1,0:T(8,128)(2,1)}, f32[16,256,512]{2,1,0:T(8,128)}, bf16[8,256,512]{2,1,0:T(8,128)(2,1)}, bf16[8,256,512]{2,1,0:T(8,128)(2...) custom-call(s32[1]{0:T(128)} %bitcast.core, s32[16]{0:T(128)} %counts.3, s32[16]{0:T(128)} %groups.3, ...), custom_call_target="tpu_custom_call" | custom-call | tf_op jit(solution)/shard_map/pallas_call | solution.py:419
  79.6 0.8 collective-permute-start.3
  80.3 0.1 collective-permute-start.4
  80.4 0.4 collective-permute-start.6
  80.8 3.6 %collective-permute-done.6.recv = f32[16,512]{1,0:T(8,128)S(1)} collective-permute-done((f32[16,512]{1,0:T(8,128)}, f32[16,512]{1,0:T(8,128)S(1)}, u32[]{:S(2)}, u32[]{:S(2)}) %collective-permute-start.6) | collective-permute-done | bytes 32800 | tf_op jit(solution)/shard_map/ppermute | solution.py:528
  84.4 0.0 copy-start.6
  84.4 0.0 all-to-all-done.shard
  84.4 0.0 copy-start.3
  84.4 0.6 copy-done.6
  85.0 0.3 copy-done.3
  85.3 2.4 %shard_map.216 = bf16[8,512,128]{2,1,0:T(8,128)(2,1)} custom-call(bf16[8,384,128]{2,1,0:T(8,128)(2,1)} %copy-done.3, f32[16,512]{1,0:T(8,128)} %get-tuple-element.54.keep, f32[16,512]{1,0:T(8,128)} %copy-done.6), custom_call_target="tpu_custom_call" | custom-call | tf_op jit(solution)/shard_map/pallas_call | solution.py:484
  87.7 9.1 %all-to-all-start.1 = ((bf16[8,512,128]{2,1,0:T(8,128)(2,1)}), bf16[8,512,128]{2,1,0:T(8,128)(2,1)S(1)}, u32[]{:S(2)}, u32[]{:S(2)}) async-start(bf16[8,512,128]{2,1,0:T(8,128)(2,1)} %shard_map.216), calls=%async_computation.1 | async-start | bytes 2097152 | tf_op jit(solution)/shard_map/all_to_all | solution.py:532
  96.8 0.0 collective-permute-done.3.out_b
  96.8 0.0 collective-permute-done.4.gtok_b
  96.8 6.9 %shard_map.215 = (bf16[16,256,512]{2,1,0:T(8,128)(2,1)}, f32[16,256,512]{2,1,0:T(8,128)}) custom-call(s32[1]{0:T(128)} %bitcast.core, bf16[8,256,512]{2,1,0:T(8,128)(2,1)} %collective-permute-done.3.out_b, bf16[8,256,512]{2,1,0:T(8,128)(2,1)} %collective-permute-done.4.gtok_b, ...), custom_call_target="tpu_custom_call", output_to_operand_aliasing={{0}: (3, {}), {1}: (4, {})} | custom-call | tf_op jit(solution)/shard_map/pallas_call | solution.py:451
  103.7 19.2 %all-to-all-done.1.msg = bf16[8,512,128]{2,1,0:T(8,128)(2,1)S(1)} async-done(((bf16[8,512,128]{2,1,0:T(8,128)(2,1)}), bf16[8,512,128]{2,1,0:T(8,128)(2,1)S(1)}, u32[]{:S(2)}, u32[]{:S(2)}) %all-to-all-start.1) | async-done | bytes 1048608 | tf_op jit(solution)/shard_map/all_to_all | solution.py:532
  122.8 0.0 copy-start.1
  122.8 1.0 copy-done.1
  123.8 2.5 %shard_map.217 = (f32[7,512]{1,0:T(8,128)}, f32[1,512]{1,0:T(1,128)}, f32[2,512]{1,0:T(2,128)}, f32[2,512]{1,0:T(2,128)}, f32[512,384]{1,0:T(8,128)}, /*index=5*...) custom-call(bf16[8,512,128]{2,1,0:T(8,128)(2,1)} %copy-done.1), custom_call_target="tpu_custom_call" | custom-call | tf_op jit(solution)/shard_map/pallas_call | solution.py:520
  126.3 1.3 reduce
Async XLA Ops:
  2.8 2.6 %collective-permute-start = (bf16[3088,128]{1,0:T(8,128)(2,1)}, bf16[3088,128]{1,0:T(8,128)(2,1)S(1)}, u32[]{:S(2)}, u32[]{:S(2)}) collective-permute-start(bf16[3088,128]{1,0:T(8,128)(2,1)} %shard_map.212.buf_a), channel_id=1, source_target_pairs={{0,1},{1,0},{2,3},{3,2},{4,5},{5,4},{6,7},{7,6},{8,9},{9,8},{10,11... | collective-permute-start | bytes 2371592 | tf_op jit(solution)/shard_map/ppermute | solution.py:528
  5.4 0.9 copy-start.2
  6.3 21.6 %copy-start = (bf16[3088,128]{1,0:T(8,128)(2,1)S(1)}, bf16[3088,128]{1,0:T(8,128)(2,1)}, u32[]{:S(2)}) copy-start(bf16[3088,128]{1,0:T(8,128)(2,1)} %shard_map.212.buf_a) | copy-start | bytes 2371588
  27.1 3.4 %collective-permute-start.5 = (bf16[3072,128]{1,0:T(8,128)(2,1)}, bf16[3072,128]{1,0:T(8,128)(2,1)S(1)}, u32[]{:S(2)}, u32[]{:S(2)}) collective-permute-start(bf16[3072,128]{1,0:T(8,128)(2,1)} %get-tuple-element.53), channel_id=1, source_target_pairs={{0,1},{1,0},{2,3},{3,2},{4,5},{5,4},{6,7},{7,6},{8,9},{9,8},{10,11... | collective-permute-start | bytes 2359304 | tf_op jit(solution)/shard_map/ppermute | solution.py:528
  27.9 20.5 %collective-permute-start.1 = (bf16[3088,128]{1,0:T(8,128)(2,1)S(1)}, bf16[3088,128]{1,0:T(8,128)(2,1)S(1)}, u32[]{:S(2)}, u32[]{:S(2)}) collective-permute-start(bf16[3088,128]{1,0:T(8,128)(2,1)S(1)} %copy-done), channel_id=1, source_target_pairs={{0,2},{1,3},{2,0},{3,1},{4,6},{5,7},{6,4},{7,5},{8,10},{9,11},{10,... | collective-permute-start | bytes 2371592 | tf_op jit(solution)/shard_map/ppermute | solution.py:528
  33.0 51.4 %all-to-all-start = ((bf16[8,384,128]{2,1,0:T(8,128)(2,1)}), bf16[8,384,128]{2,1,0:T(8,128)(2,1)S(1)}, u32[]{:S(2)}, u32[]{:S(2)}) async-start(bf16[8,384,128]{2,1,0:T(8,128)(2,1)} %bitcast.1), calls=%async_computation | async-start | bytes 1572864 | tf_op jit(solution)/shard_map/all_to_all | solution.py:532
  48.4 2.3 %copy-start.4 = (bf16[3088,128]{1,0:T(8,128)(2,1)}, bf16[3088,128]{1,0:T(8,128)(2,1)S(1)}, u32[]{:S(2)}) copy-start(bf16[3088,128]{1,0:T(8,128)(2,1)S(1)} %collective-permute-done.1.buf_c) | copy-start | bytes 2371588
  48.4 2.3 %collective-permute-start.2 = (bf16[3088,128]{1,0:T(8,128)(2,1)S(1)}, bf16[3088,128]{1,0:T(8,128)(2,1)S(1)}, u32[]{:S(2)}, u32[]{:S(2)}) collective-permute-start(bf16[3088,128]{1,0:T(8,128)(2,1)S(1)} %collective-permute-done.1.buf_c), channel_id=1, source_target_pairs={{0,1},{1,0},{2,3},{3,2},{4,5},{5,4},{6,7},{7,6},{8,9},{9,8},{10,11... | collective-permute-start | bytes 2371592 | tf_op jit(solution)/shard_map/ppermute | solution.py:528
  50.7 0.9 copy-start.5
  79.6 17.2 %collective-permute-start.3 = (bf16[8,256,512]{2,1,0:T(8,128)(2,1)}, bf16[8,256,512]{2,1,0:T(8,128)(2,1)}, u32[]{:S(2)}, u32[]{:S(2)}) collective-permute-start(bf16[8,256,512]{2,1,0:T(8,128)(2,1)} %get-tuple-element.46), channel_id=1, source_target_pairs={{0,1},{1,0},{2,3},{3,2},{4,5},{5,4},{6,7},{7,6},{8,9},{9,8},{10,11... | collective-permute-start | bytes 6291464 | tf_op jit(solution)/shard_map/ppermute | solution.py:528
  80.3 16.4 %collective-permute-start.4 = (bf16[8,256,512]{2,1,0:T(8,128)(2,1)}, bf16[8,256,512]{2,1,0:T(8,128)(2,1)}, u32[]{:S(2)}, u32[]{:S(2)}) collective-permute-start(bf16[8,256,512]{2,1,0:T(8,128)(2,1)} %get-tuple-element.47), channel_id=1, source_target_pairs={{0,1},{1,0},{2,3},{3,2},{4,5},{5,4},{6,7},{7,6},{8,9},{9,8},{10,11... | collective-permute-start | bytes 6291464 | tf_op jit(solution)/shard_map/ppermute | solution.py:528
  80.4 4.0 %collective-permute-start.6 = (f32[16,512]{1,0:T(8,128)}, f32[16,512]{1,0:T(8,128)S(1)}, u32[]{:S(2)}, u32[]{:S(2)}) collective-permute-start(f32[16,512]{1,0:T(8,128)} %get-tuple-element.55), channel_id=1, source_target_pairs={{0,1},{1,0},{2,3},{3,2},{4,5},{5,4},{6,7},{7,6},{8,9},{9,8},{10,11... | collective-permute-start | bytes 98312 | tf_op jit(solution)/shard_map/ppermute | solution.py:528
  84.4 0.6 copy-start.6
  84.4 0.9 copy-start.3
  87.7 35.1 %all-to-all-start.1 = ((bf16[8,512,128]{2,1,0:T(8,128)(2,1)}), bf16[8,512,128]{2,1,0:T(8,128)(2,1)S(1)}, u32[]{:S(2)}, u32[]{:S(2)}) async-start(bf16[8,512,128]{2,1,0:T(8,128)(2,1)} %shard_map.216), calls=%async_computation.1 | async-start | bytes 2097152 | tf_op jit(solution)/shard_map/all_to_all | solution.py:532
  122.8 1.0 copy-start.1

commit v3 on v2

v3 whole, which is shorter than its diff:
```python
import functools

import jax
import jax.numpy as jnp
from jax import lax
from jax.experimental import pallas as pl
from jax.experimental.pallas import tpu as pltpu
from jax.sharding import PartitionSpec as P

EPS = 1e-06
BF, F32 = jnp.bfloat16, jnp.float32
TILE = 256
LANES = 128
PAD = 8
CHUNK = 64
VMEM_LIMIT = 12 * 1024 * 1024


def params(**more):
    return pltpu.CompilerParams(vmem_limit_bytes=VMEM_LIMIT, **more)


def struct(shape, dtype):
    return jax.ShapeDtypeStruct(shape, dtype)


def whole(shape):
    return pl.BlockSpec(shape, lambda *_: (0,) * len(shape))


def hbm():
    return pl.BlockSpec(memory_space=pltpu.HBM)


def smem():
    return pl.BlockSpec(memory_space=pltpu.SMEM)


def cost(size):
    return pl.CostEstimate(flops=0, transcendentals=0, bytes_accessed=size)


def vmem():
    return pl.BlockSpec(memory_space=pltpu.VMEM)


def lane(q):
    return slice(q * LANES, (q + 1) * LANES)


def fold(x):
    return jnp.sum(x.reshape(x.shape[0] // 8, 8, x.shape[1]), axis=0)


def pick(table, group):
    rows = table[...].astype(F32)
    value = rows[0:1]
    for r in range(1, rows.shape[0]):
        value = jnp.where(group == r, rows[r:r + 1], value)
    return value


def as_row(ref):
    return ref[...].astype(F32).reshape(1, -1)


def gelu_parts(pre):
    cdf = 0.5 + 0.5 * lax.erf(pre * 0.7071067811865476)
    density = jnp.exp(-0.5 * pre * pre) * 0.3989422804014327
    return pre * cdf, cdf + pre * density


def dot(a, b):
    return jnp.dot(a, b, preferred_element_type=F32)


def dot_t(a, b):
    return lax.dot_general(a, b, (((1,), (1,)), ((), ())), preferred_element_type=F32)


def dot_rows(a, b):
    return lax.dot_general(a, b, (((0,), (0,)), ((), ())), preferred_element_type=F32)


def place_items(n, core, counts, offs):
    end = jnp.int32(0)
    for j in range(n):
        offs[j] = end
        end = end + (counts[core[0] * n + j] + 15) // 16 * 16
    offs[n] = end
    offs[n + 1] = (end + TILE - 1) // TILE


def pack_kernel(wi, bi, wo, out):
    width, h = wi.shape
    hq, wq = h // LANES, width // LANES
    for q in range(hq):
        out[q * width:(q + 1) * width, :] = wi[:, lane(q)]
    base = hq * width
    for q in range(wq):
        out[base + q * h:base + (q + 1) * h, :] = wo[:, lane(q)]
    base += wq * h
    bias = bi[...].astype(F32).reshape(1, h)
    rows = [bias[:, lane(q)] for q in range(hq)] + [jnp.zeros((1, LANES), F32)] * (16 - hq)
    out[base:base + 16, :] = jnp.concatenate(rows, axis=0).astype(BF)


def pack(wi, bi, wo):
    rows = 2 * wi.size // LANES + 16
    return pl.pallas_call(pack_kernel, out_shape=struct((rows, LANES), BF),
                          compiler_params=params())(wi, bi, wo)


def weight_copies(buf, side, win, wout, bias, sems):
    width, h = win.shape[0], win.shape[1] // 2
    hq, wq = h // LANES, width // LANES
    copies = []
    for q in range(hq):
        at = side * h + q * LANES
        copies.append((buf.at[pl.ds(q * width, width), :], win.at[:, pl.ds(at, LANES)]))
    base = hq * width
    for q in range(wq):
        copies.append((buf.at[pl.ds(base + q * h, h), :], wout.at[pl.ds(side * h, h), pl.ds(q * LANES, LANES)]))
    copies.append((buf.at[pl.ds(base + wq * h, 16), :], bias.at[side]))
    return [pltpu.make_async_copy(src, dst, sems.at[side, i]) for i, (src, dst) in enumerate(copies)]


def spread_bias(bias, row):
    hq = row.shape[1] // LANES // 2
    for side in range(2):
        for q in range(hq):
            at = side * hq + q
            row[:, lane(at)] = bias[side, q:q + 1, :].astype(F32)


def conv_norm_kernel(n, core, counts, groups, tok, cot, cw, cb, ns, nsh, gamma, ad, nrm, low, inv, gbo, offs, pad):
    s = pl.program_id(0)
    frames, width = tok.shape[1], tok.shape[2]
    taps = cw.shape[0]
    half = taps // 2
    wq = width // LANES

    @pl.when(s == 0)
    def _():
        place_items(n, core, counts, offs)
        gbo[...] = jnp.zeros_like(gbo)
        pad[...] = jnp.zeros_like(pad)

    item = core[0] * n + s
    count = counts[item]
    group = groups[item]
    off = offs[s]
    rows = lax.broadcasted_iota(jnp.int32, (frames, 1), 0)
    for q in range(wq):
        pad[q, PAD:PAD + frames, :] = jnp.where(rows < count, tok[0, :, lane(q)].astype(F32), 0.0)
    scale, shift = pick(ns, group), pick(nsh, group)
    gam, conv_bias = as_row(gamma), as_row(cb)
    w = cw[...].astype(F32)

    def step(i, acc):
        r0 = pl.multiple_of(i * CHUNK, CHUNK)
        live = (lax.broadcasted_iota(jnp.int32, (CHUNK, 1), 0) + r0) < count
        convs = []
        for q in range(wq):
            conv = conv_bias[:, lane(q)]
            for k in range(taps):
                conv = conv + w[k:k + 1, lane(q)] * pad[q, pl.ds(r0 + (PAD - half + k), CHUNK), :]
            convs.append(conv)
        mean = jnp.sum(sum(convs[1:], convs[0]), axis=-1, keepdims=True) * (1.0 / width)
        cents = [c - mean for c in convs]
        sq = [c * c for c in cents]
        var = jnp.sum(sum(sq[1:], sq[0]), axis=-1, keepdims=True) * (1.0 / width)
        istd = lax.rsqrt(var + EPS)
        dst = pl.ds(pl.multiple_of(off + r0, 16), CHUNK)
        inv[dst, :] = jnp.broadcast_to(istd, (CHUNK, LANES))
        new = []
        for q in range(wq):
            normed = cents[q] * istd
            ad[dst, lane(q)] = (normed * scale[:, lane(q)] + shift[:, lane(q)]).astype(BF)
            nrm[dst, lane(q)] = normed.astype(BF)
            back = jnp.where(live, cot[0, pl.ds(r0, CHUNK), lane(q)].astype(F32), 0.0) * gam[:, lane(q)]
            low[dst, lane(q)] = back.astype(BF)
            new.append(acc[q] + fold(back))
        return tuple(new)

    accs = lax.fori_loop(0, pl.cdiv(count, CHUNK), step, (jnp.zeros((8, LANES), F32),) * wq)
    for q in range(wq):
        gbo[:, lane(q)] += accs[q]

    @pl.when(s == n - 1)
    def _():
        end = pl.ds(pl.multiple_of(offs[n], 16), TILE)
        ad[end, :] = jnp.zeros((TILE, width), BF)
        low[end, :] = jnp.zeros((TILE, width), BF)


def conv_norm(core, counts, groups, tok, cot, cw, cb, ns, nsh, gamma):
    items, frames, width = tok.shape
    n = items // 2
    rows = n * frames + TILE
    item = pl.BlockSpec((1, frames, width), lambda s, c, *_: (c[0] * n + s, 0, 0))
    return pl.pallas_call(
        functools.partial(conv_norm_kernel, n),
        grid_spec=pltpu.PrefetchScalarGridSpec(
            num_scalar_prefetch=3, grid=(n,),
            in_specs=[item, item] + [whole(v.shape) for v in (cw, cb, ns, nsh, gamma)],
            out_specs=[vmem()] * 5,
            scratch_shapes=[pltpu.SMEM((n + 2,), jnp.int32),
                            pltpu.VMEM((width // LANES, frames + 4 * PAD, LANES), F32)]),
        out_shape=[struct((rows, width), BF)] * 3 + [struct((rows, LANES), F32), struct((8, width), F32)],
        compiler_params=params(), cost_estimate=cost(0),
    )(core, counts, groups, tok, cot, cw, cb, ns, nsh, gamma)


def hidden_kernel(n, core, counts, ad, low, buf_a, buf_b, act, pre, win, wout, keep, send, gbi,
                  offs, bias, bias_row, dwo, dwi, sems):
    width, h = win.shape[0], win.shape[1] // 2
    wq = width // LANES
    copies = weight_copies(buf_a, 0, win, wout, bias, sems) + weight_copies(buf_b, 1, win, wout, bias, sems)
    for c in copies:
        c.start()
    place_items(n, core, counts, offs)
    dwo[...] = jnp.zeros_like(dwo)
    dwi[...] = jnp.zeros_like(dwi)
    gbi[...] = jnp.zeros_like(gbi)
    for c in copies:
        c.wait()
    spread_bias(bias, bias_row)

    def tile(t, _):
        at = pl.ds(pl.multiple_of(t * TILE, TILE), TILE)
        a, b = ad[at, :], low[at, :]
        activation, slope = gelu_parts(dot(a, win[...]) + bias_row[...])
        grad = dot_t(b, wout[...]) * slope
        lo = activation.astype(BF)
        act[at, :] = lo
        dwo[...] += dot_rows(lo, b)
        gbi[...] += fold(grad)
        g = grad.astype(BF)
        pre[at, :] = g
        dwi[...] += dot_rows(a, g)
        return 0

    lax.fori_loop(0, offs[n + 1], tile, 0)
    for side, dst in ((0, keep), (1, send)):
        for q in range(wq):
            dst[q * h:(q + 1) * h, :] = dwo[side * h:(side + 1) * h, lane(q)].astype(dst.dtype)
        base = wq * h
        for q in range(h // LANES):
            dst[base + q * width:base + (q + 1) * width, :] = dwi[:, lane(side * (h // LANES) + q)].astype(dst.dtype)


def hidden(core, counts, ad, low, buf_a, buf_b, h, n):
    rows, width = ad.shape
    packed = 2 * width * h // LANES
    wq, hq = width // LANES, h // LANES
    return pl.pallas_call(
        functools.partial(hidden_kernel, n),
        in_specs=[smem(), smem(), vmem(), vmem(), hbm(), hbm()],
        out_specs=[vmem()] * 7,
        scratch_shapes=[pltpu.SMEM((n + 2,), jnp.int32),
                        pltpu.VMEM((2, 16, LANES), BF), pltpu.VMEM((1, 2 * h), F32),
                        pltpu.VMEM((2 * h, width), F32), pltpu.VMEM((width, 2 * h), F32),
                        pltpu.SemaphoreType.DMA((2, hq + wq + 1))],
        out_shape=[struct((rows, 2 * h), BF)] * 2 + [struct((width, 2 * h), BF), struct((2 * h, width), BF)]
        + [struct((packed, LANES), F32), struct((packed, LANES), BF), struct((8, 2 * h), F32)],
        compiler_params=params(), cost_estimate=cost(0),
    )(core, counts, ad, low, buf_a, buf_b)


def combine_kernel(dp, core, keep, recv, stay, leave):
    m = keep.shape[0] // dp
    for d in range(dp):
        src = pl.ds(pl.multiple_of((core[1] ^ d) * m, m), m)
        total = keep[src, :] + recv[src, :].astype(F32)
        dst = leave if d % 2 else stay
        dst[d // 2 * m:(d // 2 + 1) * m, :] = total.astype(dst.dtype)


def combine(core, keep, recv, dp):
    rows = keep.shape[0] // 2
    return pl.pallas_call(
        functools.partial(combine_kernel, dp),
        in_specs=[smem(), vmem(), vmem()], out_specs=[vmem(), vmem()],
        out_shape=[struct((rows, LANES), F32), struct((rows, LANES), BF)],
        compiler_params=params())(core, keep, recv)


def mix_kernel(n, core, counts, ad, low, act, pre, win1, wout1, bout, buf_c, buf_d, branch, ag,
               offs, win2, wout2, bias, bias_row, sems):
    copies = weight_copies(buf_c, 0, win2, wout2, bias, sems) + weight_copies(buf_d, 1, win2, wout2, bias, sems)
    for c in copies:
        c.start()
    place_items(n, core, counts, offs)
    for c in copies:
        c.wait()
    spread_bias(bias, bias_row)

    def tile(t, _):
        at = pl.ds(pl.multiple_of(t * TILE, TILE), TILE)
        a, b = ad[at, :], low[at, :]
        activation, slope = gelu_parts(dot(a, win2[...]) + bias_row[...])
        grad = dot_t(b, wout2[...]) * slope
        branch[at, :] = (dot(act[at, :], wout1[...]) + dot(activation.astype(BF), wout2[...])) + as_row(bout)
        ag[at, :] = dot_t(pre[at, :], win1[...]) + dot_t(grad.astype(BF), win2[...])
        return 0

    lax.fori_loop(0, offs[n + 1], tile, 0)


def mix(core, counts, ad, low, act, pre, win, wout, bout, buf_c, buf_d, n):
    rows, width = ad.shape
    h = act.shape[1] // 2
    wq, hq = width // LANES, h // LANES
    return pl.pallas_call(
        functools.partial(mix_kernel, n),
        in_specs=[smem(), smem()] + [vmem()] * 7 + [hbm()] * 2,
        out_specs=[vmem(), vmem()],
        scratch_shapes=[pltpu.SMEM((n + 2,), jnp.int32),
                        pltpu.VMEM((width, 2 * h), BF), pltpu.VMEM((2 * h, width), BF),
                        pltpu.VMEM((2, 16, LANES), BF), pltpu.VMEM((1, 2 * h), F32),
                        pltpu.SemaphoreType.DMA((2, hq + wq + 1))],
        out_shape=[struct((rows, width), F32)] * 2,
        compiler_params=params(), cost_estimate=cost(0),
    )(core, counts, ad, low, act, pre, win, wout, bout, buf_c, buf_d)


def finish_kernel(n, first, last_part, core, counts, groups, tok, cot, branch, ag, nrm, inv, sums_in, gbo, gbi, cw, ns,
                  gamma, out, gtok, *rest):
    results, (offs, cgp, sums) = rest[:-3], rest[-3:]
    s = pl.program_id(0) + first
    frames, width = tok.shape[1], tok.shape[2]
    taps, rates = cw.shape[0], ns.shape[0]
    half = taps // 2
    wq = width // LANES
    h = gbi.shape[1] // 2

    @pl.when(s == first)
    def _():
        place_items(n, core, counts, offs)
        sums[...] = sums_in[...] if last_part else jnp.zeros_like(sums)
        cgp[...] = jnp.zeros_like(cgp)

    item = core[0] * n + s
    count = counts[item]
    group = groups[item]
    off = offs[s]
    scale = pick(ns, group)
    gam = as_row(gamma)
    w = cw[...].astype(F32)
    zero = jnp.zeros((8, LANES), F32)
    steps = pl.cdiv(count, CHUNK)

    def step(i, accs):
        r0 = pl.multiple_of(i * CHUNK, CHUNK)
        here = pl.ds(r0, CHUNK)
        live = (lax.broadcasted_iota(jnp.int32, (CHUNK, 1), 0) + r0) < count
        src = pl.ds(pl.multiple_of(off + r0, 16), CHUNK)
        new = []
        ngs, nrs = [], []
        for q in range(wq):
            a_ls, a_sc, a_sh = accs[3 * q:3 * q + 3]
            br = jnp.where(live, branch[src, lane(q)], 0.0)
            tk = jnp.where(live, tok[0, here, lane(q)].astype(F32), 0.0)
            out[0, here, lane(q)] = (tk + gam[:, lane(q)] * br).astype(BF)
            g = jnp.where(live, ag[src, lane(q)], 0.0)
            nr = nrm[src, lane(q)].astype(F32)
            new += [a_ls + fold(cot[0, here, lane(q)].astype(F32) * br), a_sc + fold(g * nr), a_sh + fold(g)]
            ngs.append(g * scale[:, lane(q)])
            nrs.append(nr)
        cross = [a * b for a, b in zip(ngs, nrs)]
        m1 = jnp.sum(sum(ngs[1:], ngs[0]), axis=-1, keepdims=True) * (1.0 / width)
        m2 = jnp.sum(sum(cross[1:], cross[0]), axis=-1, keepdims=True) * (1.0 / width)
        istd = inv[src, :]
        for q in range(wq):
            cg = istd * (ngs[q] - m1 - nrs[q] * m2)
            cgp[q, pl.ds(pl.multiple_of(r0 + PAD, 8), CHUNK), :] = jnp.where(live, cg, 0.0)
        return tuple(new)

    accs = lax.fori_loop(0, steps, step, (zero,) * (3 * wq))
    for q in range(wq):
        sums[taps + 1, :, lane(q)] += accs[3 * q]
        sums[taps + 2 + group, :, lane(q)] += accs[3 * q + 1]
        sums[taps + 2 + rates + group, :, lane(q)] += accs[3 * q + 2]

    def clear(i, _):
        r0 = pl.multiple_of(i * CHUNK, CHUNK)
        here = pl.ds(r0, CHUNK)
        out[0, here, :] = jnp.zeros((CHUNK, width), BF)
        gtok[0, here, :] = jnp.zeros((CHUNK, width), BF)
        for q in range(wq):
            cgp[q, pl.ds(pl.multiple_of(r0 + PAD, 8), CHUNK), :] = jnp.zeros((CHUNK, LANES), F32)
        return 0

    lax.fori_loop(steps, frames // CHUNK, clear, 0)

    for q in range(wq):
        wl = w[:, lane(q)]

        def conv_step(i, accs):
            r0 = pl.multiple_of(i * CHUNK, CHUNK)
            here = pl.ds(r0, CHUNK)
            live = (lax.broadcasted_iota(jnp.int32, (CHUNK, 1), 0) + r0) < count
            tk = jnp.where(live, tok[0, here, lane(q)].astype(F32), 0.0)
            total = cot[0, here, lane(q)].astype(F32)
            new = []
            for k in range(taps):
                sh = cgp[q, pl.ds(r0 + (PAD + half - k), CHUNK), :]
                total = total + wl[k:k + 1] * sh
                new.append(accs[k] + fold(tk * sh))
                if k == half:
                    new_bias = accs[taps] + fold(sh)
            gtok[0, here, lane(q)] = jnp.where(live, total, 0.0).astype(BF)
            return tuple(new) + (new_bias,)

        accs = lax.fori_loop(0, steps, conv_step, (zero,) * (taps + 1))
        for k in range(taps + 1):
            sums[k, :, lane(q)] += accs[k]

    @pl.when(pl.program_id(0) == pl.num_programs(0) - 1)
    def _():
        if not last_part:
            results[0][...] = sums[...]
            return
        small_keep, small_send = results
        last = taps + 2 + 2 * rates
        rows = [jnp.sum(sums[i], axis=0, keepdims=True) for i in range(last)]
        rows.append(jnp.sum(gbo[...], axis=0, keepdims=True))
        gb = jnp.sum(gbi[...], axis=0, keepdims=True)
        fill = jnp.zeros((1, width - h), F32)
        spare = [jnp.zeros((1, width), F32)] * (small_keep.shape[0] - last - 2)
        for side, dst in ((0, small_keep), (1, small_send)):
            tail = [jnp.concatenate([gb[:, side * h:(side + 1) * h], fill], axis=1)]
            dst[...] = jnp.concatenate(rows + tail + spare, axis=0)


def finish(core, counts, groups, tok, cot, branch, ag, nrm, inv, sums, gbo, gbi, cw, ns, gamma, first, size):
    items, frames, width = tok.shape
    n = items // 2
    last_part = first + size == n
    wq = width // LANES
    taps, rates = cw.shape[0], ns.shape[0]
    n_small = -(-(taps + 4 + 2 * rates) // 8) * 8
    sums_shape = (taps + 2 + 2 * rates, 8, width)
    item = pl.BlockSpec((1, frames, width), lambda s, c, *_: (c[0] * n + first + s, 0, 0))
    mine = pl.BlockSpec((1, frames, width), lambda s, *_: (s, 0, 0))
    more = [(n_small, width)] * 2 if last_part else [sums_shape]
    if sums is None:
        sums = gbo
    return pl.pallas_call(
        functools.partial(finish_kernel, n, first, last_part),
        grid_spec=pltpu.PrefetchScalarGridSpec(
            num_scalar_prefetch=3, grid=(size,),
            in_specs=[item, item] + [vmem()] * 7 + [whole(v.shape) for v in (cw, ns, gamma)],
            out_specs=[mine, mine] + [vmem()] * len(more),
            scratch_shapes=[pltpu.SMEM((n + 2,), jnp.int32),
                            pltpu.VMEM((wq, frames + 4 * PAD, LANES), F32),
                            pltpu.VMEM(sums_shape, F32)]),
        out_shape=[struct((size, frames, width), BF)] * 2 + [struct(v, F32) for v in more],
        compiler_params=params(), cost_estimate=cost(40000000),
    )(core, counts, groups, tok, cot, branch, ag, nrm, inv, sums, gbo, gbi, cw, ns, gamma)


def merge_kernel(core, out_a, gtok_a, out_b, gtok_b, *rest):
    out, gtok = rest[-2:]

    @pl.when(pl.program_id(0) == 0)
    def _():
        out[...] = out_a[...]
        gtok[...] = gtok_a[...].astype(F32)

    @pl.when(pl.program_id(0) == 1)
    def _():
        out[...] = out_b[...]
        gtok[...] = gtok_b[...].astype(F32)


def merge(core, out_a, gtok_a, out_b, gtok_b, into, n, first, step=2):
    size, frames, width = out_a.shape
    blocks = size // step
    mine = pl.BlockSpec((step, frames, width), lambda side, s, c: (s * (1 - side) + (blocks - 1) * side, 0, 0))
    other = pl.BlockSpec((step, frames, width), lambda side, s, c: (s * side, 0, 0))
    dst = pl.BlockSpec((step, frames, width), lambda side, s, c: (((c[0] ^ side) * n + first) // step + s, 0, 0))
    return pl.pallas_call(
        merge_kernel,
        grid_spec=pltpu.PrefetchScalarGridSpec(
            num_scalar_prefetch=1, grid=(2, blocks),
            in_specs=[mine, mine, other, other] + [pl.BlockSpec(memory_space=pl.ANY)] * len(into), out_specs=[dst, dst]),
        out_shape=[struct((2 * n, frames, width), BF), struct((2 * n, frames, width), F32)],
        input_output_aliases={5: 0, 6: 1} if into else {},
        compiler_params=params(), cost_estimate=cost(20000000),
    )(core, out_a, gtok_a, out_b, gtok_b, *into)


def unpack_kernel(dp, taps, rates, core, mess_a, mess_b, small, gcw, gcb, gns, gnsh, gwi, gbi, gwo, gbo, gls, full):
    h, width = gwo.shape
    wq, hq = width // LANES, h // LANES
    m = full.shape[0] // dp
    half = m // 2
    for part, mess, order in ((0, mess_a, spread_order(dp, False)), (1, mess_b, spread_order(dp, True))):
        for i, d in enumerate(order):
            at = pl.multiple_of((core[1] ^ d) * m + part * half, half)
            full[pl.ds(at, half), :] = mess[i * half:(i + 1) * half, :].astype(F32)
    for q in range(wq):
        gwo[:, lane(q)] = full[q * h:(q + 1) * h, :]
    base = wq * h
    for q in range(hq):
        gwi[:, lane(q)] = full[base + q * width:base + (q + 1) * width, :]
    gcw[...] = small[:taps]
    gcb[...] = small[taps]
    gls[...] = small[taps + 1]
    gns[...] = small[taps + 2:taps + 2 + rates]
    gnsh[...] = small[taps + 2 + rates:taps + 2 + 2 * rates]
    at = taps + 2 + 2 * rates
    gbo[...] = small[at]
    gbi[...] = small[at + 1, :h]


def unpack(core, mess_a, mess_b, small, dp, taps, rates, width, h):
    shapes = [(taps, width), (width,), (rates, width), (rates, width), (width, h), (h,), (h, width), (width,), (width,)]
    return pl.pallas_call(
        functools.partial(unpack_kernel, dp, taps, rates), in_specs=[smem(), vmem(), vmem(), vmem()],
        out_shape=[struct(s, F32) for s in shapes],
        scratch_shapes=[pltpu.VMEM((2 * width * h // LANES, LANES), F32)],
        compiler_params=params())(core, mess_a, mess_b, small)


def swap(x, step):
    size = lax.axis_size("tp")
    return lax.ppermute(x, "tp", [(i, i ^ step) for i in range(size)])


def across(x, step):
    size = lax.axis_size("dp")
    return lax.ppermute(x, "dp", [(i, i ^ step) for i in range(size)])


def spread_steps(dp, second):
    far = [1 << i for i in range(dp.bit_length() - 2, 0, -1)]
    return [1] + far if second else far + [1]


def spread_order(dp, second):
    order = [0]
    for step in spread_steps(dp, second):
        order = order + [d ^ step for d in order]
    return order


def split(x):
    high = lax.reduce_precision(x, 8, 7)
    low = lax.reduce_precision(x - high, 8, 7)
    return jnp.concatenate([high, low], axis=0).astype(BF), high + low


def per_device(tokens, frame_counts, rate_groups, conv_weight, conv_bias, norm_scale, norm_shift,
               weight_in, bias_in, weight_out, bias_out, layer_scale, cotangent):
    width, h = weight_in.shape
    n = tokens.shape[0] // 2
    tokens = pltpu.with_memory_space_constraint(tokens, pltpu.HBM)
    cotangent = pltpu.with_memory_space_constraint(cotangent, pltpu.HBM)
    taps, rates = conv_weight.shape[0], norm_scale.shape[0]
    dp = lax.axis_size("dp")
    core = jnp.stack([lax.axis_index("tp") & 1, lax.axis_index("dp")]).astype(jnp.int32)

    buf_a = pack(weight_in, bias_in, weight_out)
    buf_b = swap(buf_a, 1)
    buf_c = swap(buf_a, 2)
    buf_d = swap(buf_c, 1)
    ad, nrm, low, inv, gbo = conv_norm(core, frame_counts, rate_groups, tokens, cotangent, conv_weight, conv_bias,
                                       norm_scale, norm_shift, layer_scale)
    act, pre, win, wout, keep, send, gbi = hidden(core, frame_counts, ad, low, buf_a, buf_b, h, n)
    stay, leave = combine(core, keep, swap(send, 1), dp)
    arrived = across(leave, 1)
    branch, ag = mix(core, frame_counts, ad, low, act, pre, win, wout, bias_out, buf_c, buf_d, n)
    arrived, branch = lax.optimization_barrier((arrived, branch))
    stay = (stay + arrived.astype(F32)).reshape(dp // 2, -1, LANES)
    pieces = [across(stay[d].astype(BF), 2 * d) for d in range(1, dp // 2)]

    def finish_part(sums, branch, first):
        return finish(core, frame_counts, rate_groups, tokens, cotangent, branch, ag, nrm, inv, sums,
                      gbo, gbi, conv_weight, norm_scale, layer_scale, first, n // 2)

    out_1, gtok_1, sums = finish_part(None, branch, 0)
    pieces, branch = lax.optimization_barrier((pieces, branch))
    out_2, gtok_2, small_keep, small_send = finish_part(sums, branch, n // 2)
    shard = stay[0]
    for piece in pieces:
        shard = shard + piece.astype(F32)
    shard = shard.astype(BF)
    small = small_keep + swap(small_send, 1)
    rows = small.shape[0] * width // LANES
    half = shard.shape[0] // 2
    mess_a, mess_b = shard[:half], shard[half:]
    for step_a, step_b in zip(spread_steps(dp, False), spread_steps(dp, True)):
        riding, small = split(small.reshape(rows, LANES))
        came_a = across(mess_a, step_a)
        came_b = across(jnp.concatenate([mess_b, riding], axis=0), step_b)
        k = mess_b.shape[0]
        mess_a = jnp.concatenate([mess_a, came_a], axis=0)
        mess_b = jnp.concatenate([mess_b, came_b[:k]], axis=0)
        small = small + (came_b[k:k + rows].astype(F32) + came_b[k + rows:].astype(F32))
    done = merge(core, out_1, gtok_1, swap(out_1, 1), swap(gtok_1, 1), (), n, 0)
    out, gtok = merge(core, out_2, gtok_2, swap(out_2, 1), swap(gtok_2, 1), done, n, n // 2)
    small = small.reshape(-1, width)
    gcw, gcb, gns, gnsh, gwi, gbi, gwo, gbo, gls = unpack(core, mess_a, mess_b, small, dp, taps, rates, width, h)
    return (out, gtok, gcw, gcb, gns, gnsh, gwi, gbi, gwo, gbo, gls)


def solution(mesh):
    items, copied = P("dp", None, None), P()
    in_specs = (items, P("dp"), P("dp"), copied, copied, copied, copied, P(None, "tp"), P("tp"), P("tp", None),
                copied, copied, items)
    out_specs = (items, items, copied, copied, copied, copied, P(None, "tp"), P("tp"), P("tp", None), copied, copied)
    return jax.shard_map(per_device, mesh=mesh, in_specs=in_specs, out_specs=out_specs, check_vma=False)
```

time: 128 us -> 117 us (0.914)
  waiting for transfers between devices: 35.6 us -> 18.9 us
  local copies, waits for them, and re-layouts: 3.66 us -> 14.3 us
  Pallas kernels: 62.7 us -> 56.1 us
    all_to_all x2 -> x0, waiting for transfers between devices: 19.2 us -> none  [exchange(): return lax.all_to_all(x, 'dp', 0, 0)]
    ppermute x0 -> x10, waiting for transfers between devices: none -> 17 us  [across(): return lax.ppermute(x, 'dp', [(i, i ^ step) for i in range(size)])]
    ppermute x0 -> x10, starting transfers between devices: none -> 16.3 us  [across(): return lax.ppermute(x, 'dp', [(i, i ^ step) for i in range(size)])]
    all_to_all x2 -> x0, starting transfers between devices: 16 us -> none  [exchange(): return lax.all_to_all(x, 'dp', 0, 0)]
    ppermute x7 -> x9, waiting for transfers between devices: 16.4 us -> 1.84 us  [swap(): return lax.ppermute(x, 'tp', [(i, i ^ step) for i in range(size)])]
    pallas_call x4 -> x7, Pallas kernels: 53.6 us -> 44 us  [the longest x2 13.7 us: finish(): pl.pallas_call(functools.partial(finish_kernel, n, first, last_part), gri...]
    unnamed x14 -> x48, local copies, waits for them, and re-layouts: 3.66 us -> 9.9 us
    pallas_call x1 -> x2, Pallas kernels: 6.87 us -> 11.9 us  [merge(): pl.pallas_call(merge_kernel, grid_spec=pltpu.PrefetchScalarGridSpec(num_s...]
  transfers between devices with their start and end apart: 9 -> 19, of which waited for: 5 -> 7; matrix products, arithmetic and copies ran while one was open for 2% -> 7% of each run, Pallas kernels for 29% -> 37%
where the time goes in v3:
time: 117 us; the launch traced here: 116 us
  Pallas kernels  56.1 us (48%)
  starting transfers between devices  22.1 us (19%)
  waiting for transfers between devices  18.9 us (16%)
  local copies, waits for them, and re-layouts  14.3 us (12%)
  other arithmetic  3.97 us (3%)
    ppermute x10, waiting for transfers between devices, across(): return lax.ppermute(x, 'dp', [(i, i ^ step) for i in range(size)])  17 us
    ppermute x10, starting transfers between devices, across(): return lax.ppermute(x, 'dp', [(i, i ^ step) for i in range(size)])  16.3 us
    pallas_call x2, Pallas kernels, finish(): pl.pallas_call(functools.partial(finish_kernel, n, first, last_part), gri...  13.7 us
    pallas_call x2, Pallas kernels, merge(): pl.pallas_call(merge_kernel, grid_spec=pltpu.PrefetchScalarGridSpec(num_s...  11.9 us
    pallas_call x1, Pallas kernels, mix(): pl.pallas_call(functools.partial(mix_kernel, n), in_specs=[smem(), smem()...  10.1 us
    unnamed x48, local copies, waits for them, and re-layouts  9.9 us
    pallas_call x1, Pallas kernels, conv_norm(): pl.pallas_call(functools.partial(conv_norm_kernel, n), grid_spec=pltpu.Pr...  9.87 us
    pallas_call x1, Pallas kernels, hidden(): pl.pallas_call(functools.partial(hidden_kernel, n), in_specs=[smem(), sme...  7.75 us
  transfers between devices with their start and end apart: 19, of which 7 were waited for; matrix products, arithmetic and copies ran while one was open for 7% of the time, Pallas kernels for 37%

profile of v3, /device:TPU:0, one launch (start us, length us, event | category | flops | bytes accessed | tf_op | source)
XLA Modules:
  0.0 116.2 jit_solution(13722042707897366705)
XLA Ops:
  0.7 1.0 copy-done.2
  1.6 1.0 copy-done.3
  2.6 0.7 copy-done.17
  3.3 0.1 shard_map.213.buf_a
  3.5 0.5 collective-permute-start
  4.0 2.6 %collective-permute-start.3 = (bf16[3088,128]{1,0:T(8,128)(2,1)S(1)}, bf16[3088,128]{1,0:T(8,128)(2,1)S(1)}, u32[]{:S(2)}, u32[]{:S(2)}) collective-permute-start(bf16[3088,128]{1,0:T(8,128)(2,1)S(1)} %shard_map.213.buf_a), channel_id=1, source_target_pairs={{0,2},{1,3},{2,0},{3,1},{4,6},{5,7},{6,4},{7,5},{8,10},{9,11},{10,... | collective-permute-start | bytes 2371592 | tf_op jit(solution)/shard_map/ppermute | solution.py:530
  6.5 0.1 pad_add_fusion.core
  6.6 0.7 copy-done.5
  7.3 0.7 copy-done.7
  8.0 0.7 copy-done.9
  8.7 0.7 copy-done.11
  9.3 0.7 copy-done.13
  10.0 0.7 copy-done.15
  10.7 0.7 copy-done.18
  11.4 9.9 %shard_map.212 = (bf16[2304,512]{1,0:T(8,128)(2,1)S(1)}, bf16[2304,512]{1,0:T(8,128)(2,1)S(1)}, bf16[2304,512]{1,0:T(8,128)(2,1)S(1)}, f32[2304,128]{1,0:T(8,128)S(1)}, f32[8,512]{1,0:T(8,128)S(1)}) custom-call(s32[2]{0:T(128)S(1)} %pad_add_fusion.core, s32[16]{0:T(128)S(1)} %copy-done.9, s32[16]{0:T(128)S(1)} %copy-done.13, bf16[16,256,512]{2,1,0:T(8,128)(2,1)} %tok.5, ...), custom_call_target="tpu_custom_call" | custom-call | tf_op jit(solution)/shard_map/pallas_call | solution.py:202
  21.3 0.0 copy-start.16
  21.3 7.7 %shard_map.214 = (bf16[2304,768]{1,0:T(8,128)(2,1)S(1)}, bf16[2304,768]{1,0:T(8,128)(2,1)S(1)}, bf16[512,768]{1,0:T(8,128)(2,1)S(1)}, bf16[768,512]{1,0:T(8,128)...) custom-call(s32[2]{0:T(128)S(1)} %pad_add_fusion.core, s32[16]{0:T(128)S(1)} %copy-done.10, ...), custom_call_target="tpu_custom_call" | custom-call | tf_op jit(solution)/shard_map/pallas_call | solution.py:257
  29.0 1.9 %collective-permute-start.1 = (bf16[3072,128]{1,0:T(8,128)(2,1)S(1)}, bf16[3072,128]{1,0:T(8,128)(2,1)S(1)}, u32[]{:S(2)}, u32[]{:S(2)}) collective-permute-start(bf16[3072,128]{1,0:T(8,128)(2,1)S(1)} %get-tuple-element.56), channel_id=1, source_target_pairs={{0,1},{1,0},{2,3},{3,2},{4,5},{5,4},{6,7},{7,6},{8,9},{9,8},{10,11... | collective-permute-start | bytes 2359304 | tf_op jit(solution)/shard_map/ppermute | solution.py:530
  30.9 0.1 collective-permute-start.4
  31.0 1.8 %collective-permute-done.1.recv = bf16[3072,128]{1,0:T(8,128)(2,1)S(1)} collective-permute-done((bf16[3072,128]{1,0:T(8,128)(2,1)S(1)}, bf16[3072,128]{1,0:T(8,128)(2,1)S(1)}, u32[]{:S(2)}, u32[]{:S(2)}) %collective-permute-start.1) | collective-permute-done | bytes 786464 | tf_op jit(solution)/shard_map/ppermute | solution.py:530
  32.8 0.7 shard_map.215
  33.5 1.6 %collective-permute-start.2 = (bf16[1536,128]{1,0:T(8,128)(2,1)S(1)}, bf16[1536,128]{1,0:T(8,128)(2,1)S(1)}, u32[]{:S(2)}, u32[]{:S(2)}) collective-permute-start(bf16[1536,128]{1,0:T(8,128)(2,1)S(1)} %get-tuple-element.58), channel_id=1, source_target_pairs={{0,4},{4,0},{8,12},{12,8},{16,20},{20,16},{24,28},{28,24},{1,5},{5... | collective-permute-start | bytes 1179656 | tf_op jit(solution)/shard_map/ppermute | solution.py:535
  35.1 0.0 collective-permute-done.4.buf_d
  35.1 0.0 copy-start.12
  35.1 0.0 copy-start.14
  35.1 10.1 %shard_map.216 = (f32[2304,512]{1,0:T(8,128)S(1)}, f32[2304,512]{1,0:T(8,128)S(1)}) custom-call(s32[2]{0:T(128)S(1)} %pad_add_fusion.core, s32[16]{0:T(128)S(1)} %copy-done.10, bf16[2304,512]{1,0:T(8,128)(2,1)S(1)} %get-tuple-element.53.ad, bf16[2304,512]{1,0:T(8,128)(2,1)S(1)} %get-tuple-element.54.low, bf16[2304,768]{1,0:T(8,128)(2,1)S(1)} %get-tuple-element.59.act, ...), custom_call_target="tpu_custom_call" | custom-call | tf_op jit(solution)/shard_map/pallas_call | solution.py:315
  45.3 0.1 fusion.15
  45.4 3.3 %collective-permute-start.5 = (bf16[384,128]{1,0:T(8,128)(2,1)S(1)}, bf16[384,128]{1,0:T(8,128)(2,1)S(1)}, u32[]{:S(2)}, u32[]{:S(2)}) collective-permute-start(bf16[384,128]{1,0:T(8,128)(2,1)S(1)} %get-tuple-element.101), channel_id=1, source_target_pairs={{0,8},{4,12},{8,0},{12,4},{16,24},{20,28},{24,16},{28,20},{1,9},{5... | collective-permute-start | bytes 294920 | tf_op jit(solution)/shard_map/ppermute | solution.py:535
  48.6 1.3 %collective-permute-start.6 = (bf16[384,128]{1,0:T(8,128)(2,1)S(1)}, bf16[384,128]{1,0:T(8,128)(2,1)S(1)}, u32[]{:S(2)}, u32[]{:S(2)}) collective-permute-start(bf16[384,128]{1,0:T(8,128)(2,1)S(1)} %get-tuple-element.100), channel_id=1, source_target_pairs={{0,16},{4,20},{8,24},{12,28},{16,0},{20,4},{24,8},{28,12},{1,17},{... | collective-permute-start | bytes 294920 | tf_op jit(solution)/shard_map/ppermute | solution.py:535
  50.0 1.1 collective-permute-start.7
  51.1 6.6 %shard_map.217 = (bf16[4,256,512]{2,1,0:T(8,128)(2,1)S(1)}, bf16[4,256,512]{2,1,0:T(8,128)(2,1)S(1)}, f32[13,8,512]{2,1,0:T(8,128)S(1)}) custom-call(s32[2]{0:T(128)S(1)} %pad_add_fusion.core, s32[16]{0:T(128)S(1)} %copy-done.10, s32[16]{0:T(128)S(1)} %copy-done.14, bf16[16,256,512]{2,1,0:T(8,128)(2,1)} %tok.5, bf16[16,256,512]{2,1,0:T(8,128)(2,1)} %cot.5, ...), custom_call_target="tpu_custom_call" | custom-call | bytes 40000000 | tf_op jit(solution)/shard_map/pallas_call | solution.py:450
  57.8 1.5 %collective-permute-done.6 = bf16[384,128]{1,0:T(8,128)(2,1)S(1)} collective-permute-done((bf16[384,128]{1,0:T(8,128)(2,1)S(1)}, bf16[384,128]{1,0:T(8,128)(2,1)S(1)}, u32[]{:S(2)}, u32[]{:S(2)}) %collective-permute-start.6) | collective-permute-done | bytes 98336 | tf_op jit(solution)/shard_map/ppermute | solution.py:535
  59.2 7.0 %shard_map.218 = (bf16[4,256,512]{2,1,0:T(8,128)(2,1)S(1)}, bf16[4,256,512]{2,1,0:T(8,128)(2,1)S(1)}, f32[16,512]{1,0:T(8,128)S(1)}, f32[16,512]{1,0:T(8,128)S(1)}) custom-call(s32[2]{0:T(128)S(1)} %pad_add_fusion.core, s32[16]{0:T(128)S(1)} %copy-done.10, s32[16]{0:T(128)S(1)} %copy-done.14, bf16[16,256,512]{2,1,0:T(8,128)(2,1)} %tok.5, ...), custom_call_target="tpu_custom_call" | custom-call | bytes 40000000 | tf_op jit(solution)/shard_map/pallas_call | solution.py:450
  66.3 1.0 copy-done
  67.3 0.1 fusion.2
  67.4 0.6 fusion.18
  68.0 2.3 %collective-permute-start.12 = (bf16[192,128]{1,0:T(8,128)(2,1)S(1)}, bf16[192,128]{1,0:T(8,128)(2,1)S(1)}, u32[]{:S(2)}, u32[]{:S(2)}) collective-permute-start(bf16[192,128]{1,0:T(8,128)(2,1)S(1)} %get-tuple-element.106), channel_id=1, source_target_pairs={{0,16},{4,20},{8,24},{12,28},{16,0},{20,4},{24,8},{28,12},{1,17},{... | collective-permute-start | bytes 147464 | tf_op jit(solution)/shard_map/ppermute | solution.py:535
  70.3 1.2 %collective-permute-start.16 = (bf16[320,128]{1,0:T(8,128)(2,1)S(1)}, bf16[320,128]{1,0:T(8,128)(2,1)S(1)}, u32[]{:S(2)}, u32[]{:S(2)}) collective-permute-start(bf16[320,128]{1,0:T(8,128)(2,1)S(1)} %pad_maximum_fusion.5), channel_id=1, source_target_pairs={{0,4},{4,0},{8,12},{12,8},{16,20},{20,16},{24,28},{28,24},{1,5},{5... | collective-permute-start | bytes 245768 | tf_op jit(solution)/shard_map/ppermute | solution.py:535
  71.6 1.5 %collective-permute-done.12 = bf16[192,128]{1,0:T(8,128)(2,1)S(1)} collective-permute-done((bf16[192,128]{1,0:T(8,128)(2,1)S(1)}, bf16[192,128]{1,0:T(8,128)(2,1)S(1)}, u32[]{:S(2)}, u32[]{:S(2)}) %collective-permute-start.12) | collective-permute-done | bytes 49184 | tf_op jit(solution)/shard_map/ppermute | solution.py:535
  73.1 2.1 %collective-permute-start.13 = (bf16[384,128]{1,0:T(8,128)(2,1)S(1)}, bf16[384,128]{1,0:T(8,128)(2,1)S(1)}, u32[]{:S(2)}, u32[]{:S(2)}) collective-permute-start(bf16[384,128]{1,0:T(8,128)(2,1)S(1)} %pad_maximum_fusion.4), channel_id=1, source_target_pairs={{0,8},{4,12},{8,0},{12,4},{16,24},{20,28},{24,16},{28,20},{1,9},{5... | collective-permute-start | bytes 294920 | tf_op jit(solution)/shard_map/ppermute | solution.py:535
  75.2 0.6 fusion.19
  75.8 1.8 %collective-permute-start.17 = (bf16[512,128]{1,0:T(8,128)(2,1)S(1)}, bf16[512,128]{1,0:T(8,128)(2,1)S(1)}, u32[]{:S(2)}, u32[]{:S(2)}) collective-permute-start(bf16[512,128]{1,0:T(8,128)(2,1)S(1)} %pad_maximum_fusion.3), channel_id=1, source_target_pairs={{0,16},{4,20},{8,24},{12,28},{16,0},{20,4},{24,8},{28,12},{1,17},{... | collective-permute-start | bytes 393224 | tf_op jit(solution)/shard_map/ppermute | solution.py:535
  77.6 0.5 collective-permute-start.11
  78.1 0.3 collective-permute-done.13
  78.3 0.2 collective-permute-start.9
  78.6 5.8 %collective-permute-done.17 = bf16[512,128]{1,0:T(8,128)(2,1)S(1)} collective-permute-done((bf16[512,128]{1,0:T(8,128)(2,1)S(1)}, bf16[512,128]{1,0:T(8,128)(2,1)S(1)}, u32[]{:S(2)}, u32[]{:S(2)}) %collective-permute-start.17) | collective-permute-done | bytes 131104 | tf_op jit(solution)/shard_map/ppermute | solution.py:535
  84.4 1.7 %collective-permute-start.14 = (bf16[768,128]{1,0:T(8,128)(2,1)S(1)}, bf16[768,128]{1,0:T(8,128)(2,1)S(1)}, u32[]{:S(2)}, u32[]{:S(2)}) collective-permute-start(bf16[768,128]{1,0:T(8,128)(2,1)S(1)} %pad_maximum_fusion.2), channel_id=1, source_target_pairs={{0,4},{4,0},{8,12},{12,8},{16,20},{20,16},{24,28},{28,24},{1,5},{5... | collective-permute-start | bytes 589832 | tf_op jit(solution)/shard_map/ppermute | solution.py:535
  86.1 0.7 fusion.17
  86.8 0.6 fusion.13
  87.4 0.6 fusion.12
  88.0 2.6 %collective-permute-done.14 = bf16[768,128]{1,0:T(8,128)(2,1)S(1)} collective-permute-done((bf16[768,128]{1,0:T(8,128)(2,1)S(1)}, bf16[768,128]{1,0:T(8,128)(2,1)S(1)}, u32[]{:S(2)}, u32[]{:S(2)}) %collective-permute-start.14) | collective-permute-done | bytes 196640 | tf_op jit(solution)/shard_map/ppermute | solution.py:535
  90.6 0.1 collective-permute-start.18
  90.7 0.9 pad_maximum_fusion.mess_a
  91.5 5.4 %collective-permute-done.18 = bf16[896,128]{1,0:T(8,128)(2,1)S(1)} collective-permute-done((bf16[896,128]{1,0:T(8,128)(2,1)}, bf16[896,128]{1,0:T(8,128)(2,1)S(1)}, u32[]{:S(2)}, u32[]{:S(2)}) %collective-permute-start.18) | collective-permute-done | bytes 229408 | tf_op jit(solution)/shard_map/ppermute | solution.py:535
  96.9 0.7 copy-done.23
  97.6 0.6 fusion.11
  98.2 1.4 %reshape.38.small = f32[16,512]{1,0:T(8,128)} reshape(f32[64,128]{1,0:T(8,128)} %fusion.11) | data formatting | bytes 65536 | tf_op jit(solution)/shard_map/reshape | solution.py:605
  99.6 1.0 slice.79
  100.6 0.9 pad_maximum_fusion.1.mess_b
  101.6 0.0 copy-start.4
  101.6 0.7 copy-done.4
  102.3 1.9 %shard_map.221 = (f32[7,512]{1,0:T(8,128)}, f32[512]{0:T(512)}, f32[2,512]{1,0:T(2,128)}, f32[2,512]{1,0:T(2,128)}, f32[512,384]{1,0:T(8,128)}, /*index=5*/f32[3...) custom-call(s32[2]{0:T(128)S(1)} %pad_add_fusion.core, bf16[1536,128]{1,0:T(8,128)(2,1)S(1)} %pad_maximum_fusion.mess_a, ...), custom_call_target="tpu_custom_call" | custom-call | tf_op jit(solution)/shard_map/pallas_call | solution.py:521
  104.2 6.0 %shard_map.219 = (bf16[16,256,512]{2,1,0:T(8,128)(2,1)}, f32[16,256,512]{2,1,0:T(8,128)}) custom-call(s32[2]{0:T(128)S(1)} %pad_add_fusion.core, bf16[4,256,512]{2,1,0:T(8,128)(2,1)S(1)} %get-tuple-element.75.out_a, bf16[4,256,512]{2,1,0:T(8,128)(2,1)S(1)} %get-tuple-element.76.gtok_a, bf16[4,256,512]{2,1,0:T(8,128)(2,1)} %collective-permute-done.10.out_b, ...), custom_call_target="tpu_custom_call" | custom-call | bytes 20000000 | tf_op jit(solution)/shard_map/pallas_call | solution.py:484
  110.2 6.0 %shard_map.220 = (bf16[16,256,512]{2,1,0:T(8,128)(2,1)}, f32[16,256,512]{2,1,0:T(8,128)}) custom-call(s32[2]{0:T(128)S(1)} %pad_add_fusion.core, bf16[4,256,512]{2,1,0:T(8,128)(2,1)S(1)} %get-tuple-element.73.out_a, bf16[4,256,512]{2,1,0:T(8,128)(2,1)S(1)} %copy-done.1, ...), custom_call_target="tpu_custom_call", output_to_operand_aliasing={{0}: (5, {}), {1}: (6, {})} | custom-call | bytes 20000000 | tf_op jit(solution)/shard_map/pallas_call | solution.py:484
  (55 shorter events, 0.2 us)
Async XLA Ops:
  0.6 1.0 copy-start.2
  1.6 1.0 copy-start.3
  2.6 0.7 copy-start.17
  3.5 17.8 %collective-permute-start = (bf16[3088,128]{1,0:T(8,128)(2,1)S(1)}, bf16[3088,128]{1,0:T(8,128)(2,1)S(1)}, u32[]{:S(2)}, u32[]{:S(2)}) collective-permute-start(bf16[3088,128]{1,0:T(8,128)(2,1)S(1)} %shard_map.213.buf_a), channel_id=1, source_target_pairs={{0,1},{1,0},{2,3},{3,2},{4,5},{5,4},{6,7},{7,6},{8,9},{9,8},{10,11... | collective-permute-start | bytes 2371592 | tf_op jit(solution)/shard_map/ppermute | solution.py:530
  4.0 27.0 %collective-permute-start.3 = (bf16[3088,128]{1,0:T(8,128)(2,1)S(1)}, bf16[3088,128]{1,0:T(8,128)(2,1)S(1)}, u32[]{:S(2)}, u32[]{:S(2)}) collective-permute-start(bf16[3088,128]{1,0:T(8,128)(2,1)S(1)} %shard_map.213.buf_a), channel_id=1, source_target_pairs={{0,2},{1,3},{2,0},{3,1},{4,6},{5,7},{6,4},{7,5},{8,10},{9,11},{10,... | collective-permute-start | bytes 2371592 | tf_op jit(solution)/shard_map/ppermute | solution.py:530
  6.6 0.7 copy-start.5
  7.3 0.7 copy-start.7
  8.0 0.7 copy-start.9
  8.7 0.7 copy-start.11
  9.3 0.7 copy-start.13
  10.0 0.7 copy-start.15
  10.7 0.7 copy-start.18
  11.4 9.9 %copy-start.10 = (s32[16]{0:T(128)S(1)}, s32[16]{0:T(128)}, u32[]{:S(2)}) copy-start(s32[16]{0:T(128)} %counts.9) | copy-start | bytes 196
  21.3 13.8 %copy-start.16 = (bf16[512]{0:T(512)(128)(2,1)S(1)}, bf16[512]{0:T(512)(128)(2,1)}, u32[]{:S(2)}) copy-start(bf16[512]{0:T(512)(128)(2,1)} %bout.1) | copy-start | bytes 3076
  29.0 3.8 %collective-permute-start.1 = (bf16[3072,128]{1,0:T(8,128)(2,1)S(1)}, bf16[3072,128]{1,0:T(8,128)(2,1)S(1)}, u32[]{:S(2)}, u32[]{:S(2)}) collective-permute-start(bf16[3072,128]{1,0:T(8,128)(2,1)S(1)} %get-tuple-element.56), channel_id=1, source_target_pairs={{0,1},{1,0},{2,3},{3,2},{4,5},{5,4},{6,7},{7,6},{8,9},{9,8},{10,11... | collective-permute-start | bytes 2359304 | tf_op jit(solution)/shard_map/ppermute | solution.py:530
  30.9 4.1 %collective-permute-start.4 = (bf16[3088,128]{1,0:T(8,128)(2,1)S(1)}, bf16[3088,128]{1,0:T(8,128)(2,1)S(1)}, u32[]{:S(2)}, u32[]{:S(2)}) collective-permute-start(bf16[3088,128]{1,0:T(8,128)(2,1)S(1)} %collective-permute-done.3.buf_c), channel_id=1, source_target_pairs={{0,1},{1,0},{2,3},{3,2},{4,5},{5,4},{6,7},{7,6},{8,9},{9,8},{10,11... | collective-permute-start | bytes 2371592 | tf_op jit(solution)/shard_map/ppermute | solution.py:530
  33.5 11.7 %collective-permute-start.2 = (bf16[1536,128]{1,0:T(8,128)(2,1)S(1)}, bf16[1536,128]{1,0:T(8,128)(2,1)S(1)}, u32[]{:S(2)}, u32[]{:S(2)}) collective-permute-start(bf16[1536,128]{1,0:T(8,128)(2,1)S(1)} %get-tuple-element.58), channel_id=1, source_target_pairs={{0,4},{4,0},{8,12},{12,8},{16,20},{20,16},{24,28},{28,24},{1,5},{5... | collective-permute-start | bytes 1179656 | tf_op jit(solution)/shard_map/ppermute | solution.py:535
  35.1 16.0 %copy-start.6 = (bf16[7,512]{1,0:T(8,128)(2,1)S(1)}, bf16[7,512]{1,0:T(8,128)(2,1)}, u32[]{:S(2)}) copy-start(bf16[7,512]{1,0:T(8,128)(2,1)} %cw.5) | copy-start | bytes 21508
  35.1 16.0 %copy-start.8 = (bf16[2,512]{1,0:T(2,128)(2,1)S(1)}, bf16[2,512]{1,0:T(2,128)(2,1)}, u32[]{:S(2)}) copy-start(bf16[2,512]{1,0:T(2,128)(2,1)} %ns.5) | copy-start | bytes 6148
  35.1 16.0 %copy-start.12 = (bf16[512]{0:T(512)(128)(2,1)S(1)}, bf16[512]{0:T(512)(128)(2,1)}, u32[]{:S(2)}) copy-start(bf16[512]{0:T(512)(128)(2,1)} %gamma.5) | copy-start | bytes 3076
  35.1 16.0 %copy-start.14 = (s32[16]{0:T(128)S(1)}, s32[16]{0:T(128)}, u32[]{:S(2)}) copy-start(s32[16]{0:T(128)} %groups.5) | copy-start | bytes 196
  45.4 12.4 %collective-permute-start.5 = (bf16[384,128]{1,0:T(8,128)(2,1)S(1)}, bf16[384,128]{1,0:T(8,128)(2,1)S(1)}, u32[]{:S(2)}, u32[]{:S(2)}) collective-permute-start(bf16[384,128]{1,0:T(8,128)(2,1)S(1)} %get-tuple-element.101), channel_id=1, source_target_pairs={{0,8},{4,12},{8,0},{12,4},{16,24},{20,28},{24,16},{28,20},{1,9},{5... | collective-permute-start | bytes 294920 | tf_op jit(solution)/shard_map/ppermute | solution.py:535
  48.6 10.6 %collective-permute-start.6 = (bf16[384,128]{1,0:T(8,128)(2,1)S(1)}, bf16[384,128]{1,0:T(8,128)(2,1)S(1)}, u32[]{:S(2)}, u32[]{:S(2)}) collective-permute-start(bf16[384,128]{1,0:T(8,128)(2,1)S(1)} %get-tuple-element.100), channel_id=1, source_target_pairs={{0,16},{4,20},{8,24},{12,28},{16,0},{20,4},{24,8},{28,12},{1,17},{... | collective-permute-start | bytes 294920 | tf_op jit(solution)/shard_map/ppermute | solution.py:535
  50.0 9.3 %collective-permute-start.7 = (bf16[384,128]{1,0:T(8,128)(2,1)S(1)}, bf16[384,128]{1,0:T(8,128)(2,1)S(1)}, u32[]{:S(2)}, u32[]{:S(2)}) collective-permute-start(bf16[384,128]{1,0:T(8,128)(2,1)S(1)} %get-tuple-element.99), channel_id=1, source_target_pairs={{0,24},{4,28},{8,16},{12,20},{16,8},{20,12},{24,0},{28,4},{1,25},{... | collective-permute-start | bytes 294920 | tf_op jit(solution)/shard_map/ppermute | solution.py:535
  66.3 1.0 copy-start
  67.3 3.0 %collective-permute-start.15 = (f32[16,512]{1,0:T(8,128)S(1)}, f32[16,512]{1,0:T(8,128)S(1)}, u32[]{:S(2)}, u32[]{:S(2)}) collective-permute-start(f32[16,512]{1,0:T(8,128)S(1)} %get-tuple-element.85), channel_id=1, source_target_pairs={{0,1},{1,0},{2,3},{3,2},{4,5},{5,4},{6,7},{7,6},{8,9},{9,8},{10,11... | collective-permute-start | bytes 98312 | tf_op jit(solution)/shard_map/ppermute | solution.py:530
  68.0 22.6 %copy-start.19 = (bf16[192,128]{1,0:T(8,128)(2,1)}, bf16[192,128]{1,0:T(8,128)(2,1)S(1)}, u32[]{:S(2)}) copy-start(bf16[192,128]{1,0:T(8,128)(2,1)S(1)} %get-tuple-element.104) | copy-start | bytes 147460
  68.0 22.6 %copy-start.20 = (bf16[192,128]{1,0:T(8,128)(2,1)}, bf16[192,128]{1,0:T(8,128)(2,1)S(1)}, u32[]{:S(2)}) copy-start(bf16[192,128]{1,0:T(8,128)(2,1)S(1)} %get-tuple-element.106) | copy-start | bytes 147460
  68.0 5.1 %collective-permute-start.12 = (bf16[192,128]{1,0:T(8,128)(2,1)S(1)}, bf16[192,128]{1,0:T(8,128)(2,1)S(1)}, u32[]{:S(2)}, u32[]{:S(2)}) collective-permute-start(bf16[192,128]{1,0:T(8,128)(2,1)S(1)} %get-tuple-element.106), channel_id=1, source_target_pairs={{0,16},{4,20},{8,24},{12,28},{16,0},{20,4},{24,8},{28,12},{1,17},{... | collective-permute-start | bytes 147464 | tf_op jit(solution)/shard_map/ppermute | solution.py:535
  70.3 4.8 %collective-permute-start.16 = (bf16[320,128]{1,0:T(8,128)(2,1)S(1)}, bf16[320,128]{1,0:T(8,128)(2,1)S(1)}, u32[]{:S(2)}, u32[]{:S(2)}) collective-permute-start(bf16[320,128]{1,0:T(8,128)(2,1)S(1)} %pad_maximum_fusion.5), channel_id=1, source_target_pairs={{0,4},{4,0},{8,12},{12,8},{16,20},{20,16},{24,28},{28,24},{1,5},{5... | collective-permute-start | bytes 245768 | tf_op jit(solution)/shard_map/ppermute | solution.py:535
  73.1 17.5 %copy-start.21 = (bf16[192,128]{1,0:T(8,128)(2,1)}, bf16[192,128]{1,0:T(8,128)(2,1)S(1)}, u32[]{:S(2)}) copy-start(bf16[192,128]{1,0:T(8,128)(2,1)S(1)} %collective-permute-done.12) | copy-start | bytes 147460
  73.1 5.3 %collective-permute-start.13 = (bf16[384,128]{1,0:T(8,128)(2,1)S(1)}, bf16[384,128]{1,0:T(8,128)(2,1)S(1)}, u32[]{:S(2)}, u32[]{:S(2)}) collective-permute-start(bf16[384,128]{1,0:T(8,128)(2,1)S(1)} %pad_maximum_fusion.4), channel_id=1, source_target_pairs={{0,8},{4,12},{8,0},{12,4},{16,24},{20,28},{24,16},{28,20},{1,9},{5... | collective-permute-start | bytes 294920 | tf_op jit(solution)/shard_map/ppermute | solution.py:535
  75.8 14.8 %copy-start.22 = (bf16[192,128]{1,0:T(8,128)(2,1)}, bf16[192,128]{1,0:T(8,128)(2,1)S(1)}, u32[]{:S(2)}) copy-start(bf16[192,128]{1,0:T(8,128)(2,1)S(1)} %get-tuple-element.107) | copy-start | bytes 147460
  75.8 8.6 %collective-permute-start.17 = (bf16[512,128]{1,0:T(8,128)(2,1)S(1)}, bf16[512,128]{1,0:T(8,128)(2,1)S(1)}, u32[]{:S(2)}, u32[]{:S(2)}) collective-permute-start(bf16[512,128]{1,0:T(8,128)(2,1)S(1)} %pad_maximum_fusion.3), channel_id=1, source_target_pairs={{0,16},{4,20},{8,24},{12,28},{16,0},{20,4},{24,8},{28,12},{1,17},{... | collective-permute-start | bytes 393224 | tf_op jit(solution)/shard_map/ppermute | solution.py:535
  77.6 26.7 %collective-permute-start.10 = (bf16[4,256,512]{2,1,0:T(8,128)(2,1)S(1)}, bf16[4,256,512]{2,1,0:T(8,128)(2,1)}, u32[]{:S(2)}, u32[]{:S(2)}) collective-permute-start(bf16[4,256,512]{2,1,0:T(8,128)(2,1)S(1)} %get-tuple-element.75.out_a), channel_id=1, source_target_pairs={{0,1},{1,0},{2,3},{3,2},{4,5},{5,4},{6,7},{7,6},{8,9},{9,8},{10,11... | collective-permute-start | bytes 3145736 | tf_op jit(solution)/shard_map/ppermute | solution.py:530
  77.6 26.7 %collective-permute-start.11 = (bf16[4,256,512]{2,1,0:T(8,128)(2,1)S(1)}, bf16[4,256,512]{2,1,0:T(8,128)(2,1)}, u32[]{:S(2)}, u32[]{:S(2)}) collective-permute-start(bf16[4,256,512]{2,1,0:T(8,128)(2,1)S(1)} %get-tuple-element.76.gtok_a), channel_id=1, source_target_pairs={{0,1},{1,0},{2,3},{3,2},{4,5},{5,4},{6,7},{7,6},{8,9},{9,8},{10,11... | collective-permute-start | bytes 3145736 | tf_op jit(solution)/shard_map/ppermute | solution.py:530
  78.1 32.1 %collective-permute-start.8 = (bf16[4,256,512]{2,1,0:T(8,128)(2,1)S(1)}, bf16[4,256,512]{2,1,0:T(8,128)(2,1)}, u32[]{:S(2)}, u32[]{:S(2)}) collective-permute-start(bf16[4,256,512]{2,1,0:T(8,128)(2,1)S(1)} %get-tuple-element.73.out_a), channel_id=1, source_target_pairs={{0,1},{1,0},{2,3},{3,2},{4,5},{5,4},{6,7},{7,6},{8,9},{9,8},{10,11... | collective-permute-start | bytes 3145736 | tf_op jit(solution)/shard_map/ppermute | solution.py:530
  78.3 31.9 %collective-permute-start.9 = (bf16[4,256,512]{2,1,0:T(8,128)(2,1)}, bf16[4,256,512]{2,1,0:T(8,128)(2,1)}, u32[]{:S(2)}, u32[]{:S(2)}) collective-permute-start(bf16[4,256,512]{2,1,0:T(8,128)(2,1)} %copy-done), channel_id=1, source_target_pairs={{0,1},{1,0},{2,3},{3,2},{4,5},{5,4},{6,7},{7,6},{8,9},{9,8},{10,11... | collective-permute-start | bytes 3145736 | tf_op jit(solution)/shard_map/ppermute | solution.py:530
  84.4 6.2 %collective-permute-start.14 = (bf16[768,128]{1,0:T(8,128)(2,1)S(1)}, bf16[768,128]{1,0:T(8,128)(2,1)S(1)}, u32[]{:S(2)}, u32[]{:S(2)}) collective-permute-start(bf16[768,128]{1,0:T(8,128)(2,1)S(1)} %pad_maximum_fusion.2), channel_id=1, source_target_pairs={{0,4},{4,0},{8,12},{12,8},{16,20},{20,16},{24,28},{28,24},{1,5},{5... | collective-permute-start | bytes 589832 | tf_op jit(solution)/shard_map/ppermute | solution.py:535
  90.6 6.3 %collective-permute-start.18 = (bf16[896,128]{1,0:T(8,128)(2,1)}, bf16[896,128]{1,0:T(8,128)(2,1)S(1)}, u32[]{:S(2)}, u32[]{:S(2)}) collective-permute-start(bf16[896,128]{1,0:T(8,128)(2,1)} %fusion.12), channel_id=1, source_target_pairs={{0,8},{4,12},{8,0},{12,4},{16,24},{20,28},{24,16},{28,20},{1,9},{5... | collective-permute-start | bytes 688136 | tf_op jit(solution)/shard_map/ppermute | solution.py:535
  96.9 0.7 copy-start.23
  99.6 10.6 %copy-start.1 = (bf16[4,256,512]{2,1,0:T(8,128)(2,1)S(1)}, bf16[4,256,512]{2,1,0:T(8,128)(2,1)}, u32[]{:S(2)}) copy-start(bf16[4,256,512]{2,1,0:T(8,128)(2,1)} %copy-done) | copy-start | bytes 3145732
  101.6 0.8 copy-start.4
